TPU v7x, 512 devices: a whole 4x8x8 slice. The times are simulated.
512 devices in a mesh: box: 64 (over z_hi, y, core), src: 8 (over z_lo, x).
Axes of the slice: x: 4, y: 8, z: 8 (z_hi: 4, z_lo: 2; z = z_hi * 2 + z_lo), core: 2. Of those that a mesh axis runs over, the one named last changes fastest.
Arguments:
- incident: bfloat16 [512, 1024, 256], P('box', 'src'), may hold values from -6 to 6
- reflectivity: float32 [512, 128], P('box'), may hold values from 0.5 to 2
- w_self: bfloat16 [3, 512, 2, 128, 128], P(None, 'box'), may hold values from -0.25 to 0.25
- w_cross: bfloat16 [3, 512, 2, 128, 128], P(None, 'box'), may hold values from -0.25 to 0.25
- receivers: int32 [512], P('box'), may hold values from 0 to 511, as said below
- observed: bfloat16 [512, 1024, 256], P('box', 'src'), may hold values from -6 to 6
- group_of: int32 [1024], P('src'), may hold values from 0 to 15
- deltas: float32 [16], replicated, may hold values from 0.5 to 4
Outputs:
- image_grad: float32 [512, 128], P('box', 'src')
Inputs may be any that keep to these rules, and one draw needn't show every extreme that they name: `receivers`: trace t lies in box block t // 8, that is between (8 * (t // 8)) and (8 * (t // 8) + 7).
All inputs are finite; a program needn't handle non-finite values.
Results may differ from a plain program's by a relative error of at most 0.001.
Values may be sent and summed in bfloat16 or wider, within the bound.
No kernel may reach another device: no remote copies, remote signals or barrier semaphores. Data moves between devices by JAX's collectives and lax.ppermute only.
A program may use at most 64 MiB of HBM per device.

v0:
```python
import jax
import jax.numpy as jnp
from jax import lax
from jax.sharding import PartitionSpec as P


def from_partner(x, axis, distance):
    return lax.ppermute(x, axis, [(i, i ^ 1 << distance) for i in range(lax.axis_size(axis))])


def block_form(weights):
    real_part = weights[:, 0]
    imag_part = weights[:, 1]
    upper_rows = jnp.concatenate([real_part, imag_part], axis=2)
    lower_rows = jnp.concatenate([-imag_part, real_part], axis=2)
    return jnp.concatenate([upper_rows, lower_rows], axis=1)


def forward_apply(values, block):
    return jnp.einsum("bsi,bij->bsj", values, block, preferred_element_type=jnp.float32)


def adjoint_apply(values, block):
    return jnp.einsum("bsj,bij->bsi", values, block, preferred_element_type=jnp.float32)


def body(incident, reflectivity, w_self, w_cross, receivers, observed, group_of, deltas):
    box_count = incident.shape[0]
    sections = w_self.shape[0]
    top_bit = lax.axis_size("box").bit_length() - 1
    block_start = lax.axis_index("box") * box_count
    onehot = (
        (receivers - block_start)[:, None] == jnp.arange(box_count, dtype=jnp.int32)[None, :]
    ).astype(jnp.bfloat16)
    doubled = jnp.concatenate([reflectivity, reflectivity], axis=1)
    wavefield = (doubled[:, None, :] * incident.astype(jnp.float32)).astype(jnp.bfloat16)
    self_blocks = []
    cross_blocks = []
    predicted = None
    for section_idx in range(sections):
        swap_bit = top_bit - 1 - section_idx
        self_block = block_form(w_self[section_idx])
        cross_block = block_form(w_cross[section_idx])
        self_blocks.append(self_block)
        cross_blocks.append(cross_block)
        partner_field = from_partner(wavefield, "box", swap_bit)
        summed = forward_apply(wavefield, self_block) + forward_apply(partner_field, cross_block)
        wavefield = summed.astype(jnp.bfloat16)
    predicted = jnp.einsum("kb,bsi->ksi", onehot, wavefield, preferred_element_type=jnp.float32)
    residual = predicted - observed.astype(jnp.float32)
    node_count = residual.shape[2] // 2
    magnitude = residual[..., :node_count] ** 2 + residual[..., node_count:] ** 2
    group_hits = (
        group_of[:, None] == jnp.arange(deltas.shape[0], dtype=jnp.int32)[None, :]
    ).astype(jnp.float32)
    scale_src = jnp.sum(group_hits * deltas[None, :], axis=1)
    damping = 1.0 / jnp.sqrt(1.0 + magnitude / scale_src[None, :, None] ** 2)
    adj_traces = (residual * jnp.concatenate([damping, damping], axis=2)).astype(jnp.bfloat16)
    adjoint_field = jnp.einsum(
        "kb,ksi->bsi", onehot, adj_traces, preferred_element_type=jnp.float32
    ).astype(jnp.bfloat16)
    for section_idx in reversed(range(sections)):
        swap_bit = top_bit - 1 - section_idx
        outgoing = adjoint_apply(adjoint_field, cross_blocks[section_idx]).astype(jnp.bfloat16)
        received = from_partner(outgoing, "box", swap_bit)
        summed = adjoint_apply(adjoint_field, self_blocks[section_idx]) + received.astype(
            jnp.float32
        )
        adjoint_field = summed.astype(jnp.bfloat16)
    products = incident.astype(jnp.float32) * adjoint_field.astype(jnp.float32)
    image_local = jnp.sum(products[..., :node_count] + products[..., node_count:], axis=1)
    image_summed = lax.psum(image_local, "src")
    share = node_count // lax.axis_size("src")
    return lax.dynamic_slice_in_dim(image_summed, lax.axis_index("src") * share, share, 1)


def solution(mesh):
    in_specs = (
        P("box", "src", None),
        P("box", None),
        P(None, "box", None, None, None),
        P(None, "box", None, None, None),
        P("box"),
        P("box", "src", None),
        P("src"),
        P(),
    )
    out_specs = P("box", "src")
    return jax.shard_map(body, mesh=mesh, in_specs=in_specs, out_specs=out_specs, check_vma=False)
```

profile of v0, /device:TPU:104, one launch (start us, length us, event | category | flops | bytes accessed | tf_op | source)
XLA Modules:
  0.0 215.5 jit_solution(12504937117829096219)
XLA Ops:
  0.0 0.8 pad_maximum_fusion
  0.8 1.1 fusion.5
  1.9 10.0 %collective-permute-start = (bf16[8,128,256]{2,1,0:T(8,128)(2,1)S(1)}, bf16[8,128,256]{2,1,0:T(8,128)(2,1)}, u32[]{:S(2)}, u32[]{:S(2)}) collective-permute-start(bf16[8,128,256]{2,1,0:T(8,128)(2,1)S(1)} %fusion.5), channel_id=1, source_target_pairs={{0,256},{8,264},{16,272},{24,280},{32,288},{40,296},{48,304},{56,3... | collective-permute-start | bytes 1572872 | tf_op jit(solution)/shard_map/ppermute | solution.py:8
  11.9 1.5 fusion.48
  13.5 0.9 slice_bitcast_fusion.10
  14.4 0.6 copy-done
  15.2 0.8 slice_bitcast_fusion.8
  16.1 0.9 slice_bitcast_fusion.6
  17.3 0.7 fusion.47
  18.1 1.5 fusion.22
  19.6 15.9 %collective-permute-done = bf16[8,128,256]{2,1,0:T(8,128)(2,1)} collective-permute-done((bf16[8,128,256]{2,1,0:T(8,128)(2,1)S(1)}, bf16[8,128,256]{2,1,0:T(8,128)(2,1)}, u32[]{:S(2)}, u32[]{:S(2)}) %collective-permute-start) | collective-permute-done | bytes 524320 | tf_op jit(solution)/shard_map/ppermute | solution.py:8
  35.5 1.4 fusion
  36.9 1.9 collective-permute-start.1
  39.3 21.4 %collective-permute-done.1 = bf16[8,128,256]{2,1,0:T(8,128)(2,1)S(1)} collective-permute-done((bf16[8,128,256]{2,1,0:T(8,128)(2,1)S(1)}, bf16[8,128,256]{2,1,0:T(8,128)(2,1)S(1)}, u32[]{:S(2)}, u32[]{:S(2)}) %collective-permute-start.1) | collective-permute-done | bytes 524320 | tf_op jit(solution)/shard_map/ppermute | solution.py:8
  61.0 2.9 %collective-permute-start.2 = (bf16[8,128,256]{2,1,0:T(8,128)(2,1)S(1)}, bf16[8,128,256]{2,1,0:T(8,128)(2,1)S(1)}, u32[]{:S(2)}, u32[]{:S(2)}) collective-permute-start(bf16[8,128,256]{2,1,0:T(8,128)(2,1)S(1)} %fusion.1), channel_id=1, source_target_pairs={{0,64},{8,72},{16,80},{24,88},{32,96},{40,104},{48,112},{56,120},{... | collective-permute-start | bytes 1572872 | tf_op jit(solution)/shard_map/ppermute | solution.py:8
  64.4 25.1 %collective-permute-done.2 = bf16[8,128,256]{2,1,0:T(8,128)(2,1)S(1)} collective-permute-done((bf16[8,128,256]{2,1,0:T(8,128)(2,1)S(1)}, bf16[8,128,256]{2,1,0:T(8,128)(2,1)S(1)}, u32[]{:S(2)}, u32[]{:S(2)}) %collective-permute-start.2) | collective-permute-done | bytes 524320 | tf_op jit(solution)/shard_map/ppermute | solution.py:8
  89.8 0.7 copy-done.2
  90.6 1.4 convolution_subtract_fusion
  92.5 0.5 convolution_convert_fusion.2
  93.0 2.7 %collective-permute-start.3 = (bf16[8,128,256]{2,1,0:T(8,128)(2,1)S(1)}, bf16[8,128,256]{2,1,0:T(8,128)(2,1)S(1)}, u32[]{:S(2)}, u32[]{:S(2)}) collective-permute-start(bf16[8,128,256]{2,1,0:T(8,128)(2,1)S(1)} %convolution_convert_fusion.2), channel_id=1, source_target_pairs={{0,64},{8,72},{16,80},{24,88},{32,96},{40,104},{48,112},{56,120},{... | collective-permute-start | bytes 1572872 | tf_op jit(solution)/shard_map/ppermute | solution.py:8
  95.7 12.3 %collective-permute-done.3 = bf16[8,128,256]{2,1,0:T(8,128)(2,1)S(1)} collective-permute-done((bf16[8,128,256]{2,1,0:T(8,128)(2,1)S(1)}, bf16[8,128,256]{2,1,0:T(8,128)(2,1)S(1)}, u32[]{:S(2)}, u32[]{:S(2)}) %collective-permute-start.3) | collective-permute-done | bytes 524320 | tf_op jit(solution)/shard_map/ppermute | solution.py:8
  108.0 0.5 add_convert_fusion
  108.5 0.5 convolution_convert_fusion.1
  109.0 5.3 %collective-permute-start.4 = (bf16[8,128,256]{2,1,0:T(8,128)(2,1)S(1)}, bf16[8,128,256]{2,1,0:T(8,128)(2,1)S(1)}, u32[]{:S(2)}, u32[]{:S(2)}) collective-permute-start(bf16[8,128,256]{2,1,0:T(8,128)(2,1)S(1)} %convolution_convert_fusion.1), channel_id=1, source_target_pairs={{0,128},{8,136},{16,144},{24,152},{32,160},{40,168},{48,176},{56,1... | collective-permute-start | bytes 1572872 | tf_op jit(solution)/shard_map/ppermute | solution.py:8
  114.3 7.1 %collective-permute-done.4 = bf16[8,128,256]{2,1,0:T(8,128)(2,1)S(1)} collective-permute-done((bf16[8,128,256]{2,1,0:T(8,128)(2,1)S(1)}, bf16[8,128,256]{2,1,0:T(8,128)(2,1)S(1)}, u32[]{:S(2)}, u32[]{:S(2)}) %collective-permute-start.4) | collective-permute-done | bytes 524320 | tf_op jit(solution)/shard_map/ppermute | solution.py:8
  121.4 0.5 fusion.2
  122.0 0.5 convolution_convert_fusion
  122.4 14.4 %collective-permute-start.5 = (bf16[8,128,256]{2,1,0:T(8,128)(2,1)S(1)}, bf16[8,128,256]{2,1,0:T(8,128)(2,1)S(1)}, u32[]{:S(2)}, u32[]{:S(2)}) collective-permute-start(bf16[8,128,256]{2,1,0:T(8,128)(2,1)S(1)} %convolution_convert_fusion), channel_id=1, source_target_pairs={{0,256},{8,264},{16,272},{24,280},{32,288},{40,296},{48,304},{56,3... | collective-permute-start | bytes 1572872 | tf_op jit(solution)/shard_map/ppermute | solution.py:8
  136.8 14.5 %collective-permute-done.5 = bf16[8,128,256]{2,1,0:T(8,128)(2,1)S(1)} collective-permute-done((bf16[8,128,256]{2,1,0:T(8,128)(2,1)S(1)}, bf16[8,128,256]{2,1,0:T(8,128)(2,1)S(1)}, u32[]{:S(2)}, u32[]{:S(2)}) %collective-permute-start.5) | collective-permute-done | bytes 524320 | tf_op jit(solution)/shard_map/ppermute | solution.py:8
  151.3 0.5 convert_multiply_fusion
  151.9 63.0 %psum.7 = f32[8,128]{1,0:T(8,128)S(1)} all-reduce(f32[8,128]{1,0:T(8,128)S(1)} %fusion.10), channel_id=1, replica_groups=mesh['box'=64,'src'=8] {'src'}, use_global_device_ids=true, to_apply=%region_2.0 | all-reduce | flops 1024 | bytes 8192 | tf_op jit(solution)/shard_map/psum | solution.py:72
  214.8 0.7 constant_dynamic-slice_fusion
  (49 shorter events, 2.7 us)
Async XLA Ops:
  1.9 33.6 %collective-permute-start = (bf16[8,128,256]{2,1,0:T(8,128)(2,1)S(1)}, bf16[8,128,256]{2,1,0:T(8,128)(2,1)}, u32[]{:S(2)}, u32[]{:S(2)}) collective-permute-start(bf16[8,128,256]{2,1,0:T(8,128)(2,1)S(1)} %fusion.5), channel_id=1, source_target_pairs={{0,256},{8,264},{16,272},{24,280},{32,288},{40,296},{48,304},{56,3... | collective-permute-start | bytes 1572872 | tf_op jit(solution)/shard_map/ppermute | solution.py:8
  13.4 1.6 copy-start
  18.0 17.4 %copy-start.6 = (bf16[8,128,128]{2,1,0:T(8,128)(2,1)S(1)}, bf16[8,128,128]{2,1,0:T(8,128)(2,1)}, u32[]{:S(2)}) copy-start(bf16[8,128,128]{2,1,0:T(8,128)(2,1)} %get-tuple-element.19) | copy-start | bytes 786436
  18.1 17.4 %copy-start.7 = (bf16[8,128,128]{2,1,0:T(8,128)(2,1)S(1)}, bf16[8,128,128]{2,1,0:T(8,128)(2,1)}, u32[]{:S(2)}) copy-start(bf16[8,128,128]{2,1,0:T(8,128)(2,1)} %get-tuple-element.20) | copy-start | bytes 786436
  35.5 3.4 %copy-start.10 = (s32[8]{0:T(128)S(1)}, s32[8]{0:T(128)}, u32[]{:S(2)}) copy-start(s32[8]{0:T(128)} %param.12) | copy-start | bytes 100
  35.5 3.4 %copy-start.8 = (bf16[8,128,128]{2,1,0:T(8,128)(2,1)S(1)}, bf16[8,128,128]{2,1,0:T(8,128)(2,1)}, u32[]{:S(2)}) copy-start(bf16[8,128,128]{2,1,0:T(8,128)(2,1)} %get-tuple-element.17) | copy-start | bytes 786436
  35.5 3.4 %copy-start.9 = (bf16[8,128,128]{2,1,0:T(8,128)(2,1)S(1)}, bf16[8,128,128]{2,1,0:T(8,128)(2,1)}, u32[]{:S(2)}) copy-start(bf16[8,128,128]{2,1,0:T(8,128)(2,1)} %get-tuple-element.18) | copy-start | bytes 786436
  36.9 23.7 %collective-permute-start.1 = (bf16[8,128,256]{2,1,0:T(8,128)(2,1)S(1)}, bf16[8,128,256]{2,1,0:T(8,128)(2,1)S(1)}, u32[]{:S(2)}, u32[]{:S(2)}) collective-permute-start(bf16[8,128,256]{2,1,0:T(8,128)(2,1)S(1)} %fusion), channel_id=1, source_target_pairs={{0,128},{8,136},{16,144},{24,152},{32,160},{40,168},{48,176},{56,1... | collective-permute-start | bytes 1572872 | tf_op jit(solution)/shard_map/ppermute | solution.py:8
  60.6 3.3 %copy-start.11 = (f32[16]{0:T(128)S(1)}, f32[16]{0:T(128)}, u32[]{:S(2)}) copy-start(f32[16]{0:T(128)} %param.15) | copy-start | bytes 196
  60.7 3.3 %copy-start.12 = (s32[128]{0:T(128)S(1)}, s32[128]{0:T(128)}, u32[]{:S(2)}) copy-start(s32[128]{0:T(128)} %param.14) | copy-start | bytes 1540
  61.0 28.5 %collective-permute-start.2 = (bf16[8,128,256]{2,1,0:T(8,128)(2,1)S(1)}, bf16[8,128,256]{2,1,0:T(8,128)(2,1)S(1)}, u32[]{:S(2)}, u32[]{:S(2)}) collective-permute-start(bf16[8,128,256]{2,1,0:T(8,128)(2,1)S(1)} %fusion.1), channel_id=1, source_target_pairs={{0,64},{8,72},{16,80},{24,88},{32,96},{40,104},{48,112},{56,120},{... | collective-permute-start | bytes 1572872 | tf_op jit(solution)/shard_map/ppermute | solution.py:8
  64.1 25.5 %copy-start.3 = (bf16[8,128,128]{2,1,0:T(8,128)(2,1)S(1)}, bf16[8,128,128]{2,1,0:T(8,128)(2,1)}, u32[]{:S(2)}) copy-start(bf16[8,128,128]{2,1,0:T(8,128)(2,1)} %fusion.47) | copy-start | bytes 786436
  89.5 1.0 copy-start.2
  93.0 15.1 %collective-permute-start.3 = (bf16[8,128,256]{2,1,0:T(8,128)(2,1)S(1)}, bf16[8,128,256]{2,1,0:T(8,128)(2,1)S(1)}, u32[]{:S(2)}, u32[]{:S(2)}) collective-permute-start(bf16[8,128,256]{2,1,0:T(8,128)(2,1)S(1)} %convolution_convert_fusion.2), channel_id=1, source_target_pairs={{0,64},{8,72},{16,80},{24,88},{32,96},{40,104},{48,112},{56,120},{... | collective-permute-start | bytes 1572872 | tf_op jit(solution)/shard_map/ppermute | solution.py:8
  109.0 12.4 %collective-permute-start.4 = (bf16[8,128,256]{2,1,0:T(8,128)(2,1)S(1)}, bf16[8,128,256]{2,1,0:T(8,128)(2,1)S(1)}, u32[]{:S(2)}, u32[]{:S(2)}) collective-permute-start(bf16[8,128,256]{2,1,0:T(8,128)(2,1)S(1)} %convolution_convert_fusion.1), channel_id=1, source_target_pairs={{0,128},{8,136},{16,144},{24,152},{32,160},{40,168},{48,176},{56,1... | collective-permute-start | bytes 1572872 | tf_op jit(solution)/shard_map/ppermute | solution.py:8
  121.9 29.4 %copy-start.1 = (bf16[8,128,256]{2,1,0:T(8,128)(2,1)S(1)}, bf16[8,128,256]{2,1,0:T(8,128)(2,1)}, u32[]{:S(2)}) copy-start(bf16[8,128,256]{2,1,0:T(8,128)(2,1)} %param.8) | copy-start | bytes 1572868
  121.9 29.4 %copy-start.4 = (bf16[8,128,128]{2,1,0:T(8,128)(2,1)S(1)}, bf16[8,128,128]{2,1,0:T(8,128)(2,1)}, u32[]{:S(2)}) copy-start(bf16[8,128,128]{2,1,0:T(8,128)(2,1)} %get-tuple-element.21) | copy-start | bytes 786436
  121.9 29.4 %copy-start.5 = (bf16[8,128,128]{2,1,0:T(8,128)(2,1)S(1)}, bf16[8,128,128]{2,1,0:T(8,128)(2,1)}, u32[]{:S(2)}) copy-start(bf16[8,128,128]{2,1,0:T(8,128)(2,1)} %get-tuple-element.22) | copy-start | bytes 786436
  122.4 28.9 %collective-permute-start.5 = (bf16[8,128,256]{2,1,0:T(8,128)(2,1)S(1)}, bf16[8,128,256]{2,1,0:T(8,128)(2,1)S(1)}, u32[]{:S(2)}, u32[]{:S(2)}) collective-permute-start(bf16[8,128,256]{2,1,0:T(8,128)(2,1)S(1)} %convolution_convert_fusion), channel_id=1, source_target_pairs={{0,256},{8,264},{16,272},{24,280},{32,288},{40,296},{48,304},{56,3... | collective-permute-start | bytes 1572872 | tf_op jit(solution)/shard_map/ppermute | solution.py:8
where the time goes:
time: 216 us; the launch traced here: 215 us
  waiting for transfers between devices  96.3 us (45%)
  blocking collectives  63 us (29%)
  starting transfers between devices  37.3 us (17%)
  matrix products  8.74 us (4%)
  local copies, waits for them, and re-layouts  6.61 us (3%)
  other arithmetic  3.18 us (1%)
    ppermute x6, waiting for transfers between devices, from_partner(): lax.ppermute(x, axis, [(i, i ^ 1 << distance) for i in range(lax.axis_siz...  96.3 us
    psum x1, blocking collectives, body(): image_summed = lax.psum(image_local, 'src')  63 us
    ppermute x6, starting transfers between devices, from_partner(): lax.ppermute(x, axis, [(i, i ^ 1 << distance) for i in range(lax.axis_siz...  37.3 us
  transfers between devices with their start and end apart: 6, of which 6 were waited for; matrix products, arithmetic and copies ran while one was open for 4% of the time, Pallas kernels for 0%

commit v1 on v0

v1 whole, which is shorter than its diff:
```python
import jax
import jax.numpy as jnp
from jax import lax
from jax.sharding import PartitionSpec as P

CHUNKS = 2


def from_partner(x, axis, distance):
    return lax.ppermute(x, axis, [(i, i ^ 1 << distance) for i in range(lax.axis_size(axis))])


def block_form(weights):
    real_part = weights[:, 0]
    imag_part = weights[:, 1]
    upper_rows = jnp.concatenate([real_part, imag_part], axis=2)
    lower_rows = jnp.concatenate([-imag_part, real_part], axis=2)
    return jnp.concatenate([upper_rows, lower_rows], axis=1)


def forward_apply(values, block):
    return jnp.einsum("bsi,bij->bsj", values, block, preferred_element_type=jnp.float32)


def adjoint_apply(values, block):
    return jnp.einsum("bsj,bij->bsi", values, block, preferred_element_type=jnp.float32)


def image_terms(incident, adjoint):
    products = incident.astype(jnp.float32) * adjoint
    node_count = products.shape[2] // 2
    return jnp.sum(products[..., :node_count] + products[..., node_count:], axis=1)


def body(incident, reflectivity, w_self, w_cross, receivers, observed, group_of, deltas):
    box_count, source_count, width = incident.shape
    node_count = width // 2
    sections = w_self.shape[0]
    box_devices = lax.axis_size("box")
    src_devices = lax.axis_size("src")
    top_bit = box_devices.bit_length() - 1
    swap_bits = [top_bit - 1 - section for section in range(sections)]
    block_start = lax.axis_index("box") * box_count
    onehot = (
        (receivers - block_start)[:, None] == jnp.arange(box_count, dtype=jnp.int32)[None, :]
    ).astype(jnp.bfloat16)
    group_hits = (
        group_of[:, None] == jnp.arange(deltas.shape[0], dtype=jnp.int32)[None, :]
    ).astype(jnp.float32)
    scale_src = jnp.sum(group_hits * deltas[None, :], axis=1)
    step = source_count // CHUNKS
    spans = [slice(c * step, (c + 1) * step) for c in range(CHUNKS)]

    incidents = [incident[:, span] for span in spans]
    partner_incidents = [from_partner(x, "box", swap_bits[0]) for x in incidents]
    partner_reflectivity = from_partner(reflectivity, "box", swap_bits[0])
    self_blocks = [block_form(w_self[section]) for section in range(sections)]
    cross_blocks = [block_form(w_cross[section]) for section in range(sections)]

    def scaled(field, gains):
        doubled = jnp.concatenate([gains, gains], axis=1)
        return (doubled[:, None, :] * field.astype(jnp.float32)).astype(jnp.bfloat16)

    fields = [scaled(x, reflectivity) for x in incidents]
    partners = [scaled(x, partner_reflectivity) for x in partner_incidents]
    for section in range(sections):
        if section:
            partners = [from_partner(x, "box", swap_bits[section]) for x in fields]
        fields = [
            (
                forward_apply(x, self_blocks[section]) + forward_apply(p, cross_blocks[section])
            ).astype(jnp.bfloat16)
            for x, p in zip(fields, partners)
        ]
    adjoints = []
    for span, field in zip(spans, fields):
        predicted = jnp.einsum("kb,bsi->ksi", onehot, field, preferred_element_type=jnp.float32)
        residual = predicted - observed[:, span].astype(jnp.float32)
        magnitude = residual[..., :node_count] ** 2 + residual[..., node_count:] ** 2
        damping = 1.0 / jnp.sqrt(1.0 + magnitude / scale_src[None, span, None] ** 2)
        adj_traces = (residual * jnp.concatenate([damping, damping], axis=2)).astype(jnp.bfloat16)
        adjoints.append(
            jnp.einsum(
                "kb,ksi->bsi", onehot, adj_traces, preferred_element_type=jnp.float32
            ).astype(jnp.bfloat16)
        )
    for section in range(sections - 1, 0, -1):
        received = [
            from_partner(
                adjoint_apply(x, cross_blocks[section]).astype(jnp.bfloat16),
                "box",
                swap_bits[section],
            )
            for x in adjoints
        ]
        adjoints = [
            (adjoint_apply(x, self_blocks[section]) + r.astype(jnp.float32)).astype(jnp.bfloat16)
            for x, r in zip(adjoints, received)
        ]
    own = sum(
        image_terms(x, adjoint_apply(a, self_blocks[0])) for x, a in zip(incidents, adjoints)
    )
    other = sum(
        image_terms(x, adjoint_apply(a, cross_blocks[0]))
        for x, a in zip(partner_incidents, adjoints)
    )
    share = node_count // src_devices
    both = jnp.concatenate([own, other], axis=0)
    pieces = both.reshape(2 * box_count, src_devices, share).transpose(1, 0, 2)
    gathered = lax.all_to_all(pieces, "src", 0, 0)
    totals = jnp.sum(gathered, axis=0)
    return totals[:box_count] + from_partner(totals[box_count:], "box", swap_bits[0])


def solution(mesh):
    in_specs = (
        P("box", "src", None),
        P("box", None),
        P(None, "box", None, None, None),
        P(None, "box", None, None, None),
        P("box"),
        P("box", "src", None),
        P("src"),
        P(),
    )
    out_specs = P("box", "src")
    return jax.shard_map(body, mesh=mesh, in_specs=in_specs, out_specs=out_specs, check_vma=False)
```

time: 216 us -> 159 us (0.74)
  the two profiles are of different devices: /device:TPU:104 before, /device:TPU:16 now
where the time goes in v1:
time: 159 us; the launch traced here: 158 us
  starting transfers between devices  59.9 us (38%)
  waiting for transfers between devices  58.6 us (37%)
  matrix products  15.8 us (10%)
  local copies, waits for them, and re-layouts  10.4 us (7%)
  blocking collectives  10.3 us (6%)
  other arithmetic  2.12 us (1%)
    ppermute x12, starting transfers between devices, from_partner(): lax.ppermute(x, axis, [(i, i ^ 1 << distance) for i in range(lax.axis_siz...  59.9 us
    ppermute x12, waiting for transfers between devices, from_partner(): lax.ppermute(x, axis, [(i, i ^ 1 << distance) for i in range(lax.axis_siz...  58.6 us
    all_to_all x1, blocking collectives, body(): gathered = lax.all_to_all(pieces, 'src', 0, 0)  10.3 us
    dot_general x12, matrix products, forward_apply(): jnp.einsum('bsi,bij->bsj', values, block, preferred_element_type=jnp.floa...  7.5 us
    dot_general x12, matrix products, adjoint_apply(): jnp.einsum('bsj,bij->bsi', values, block, preferred_element_type=jnp.floa...  7.22 us
    squeeze x6, local copies, waits for them, and re-layouts, block_form(): imag_part = weights[:, 1]  4.1 us
  transfers between devices with their start and end apart: 12, of which 9 were waited for; matrix products, arithmetic and copies ran while one was open for 12% of the time, Pallas kernels for 0%

profile of v1, /device:TPU:16, one launch (start us, length us, event | category | flops | bytes accessed | tf_op | source)
XLA Modules:
  0.0 157.8 jit_solution(16627227575178554258)
XLA Ops:
  0.0 1.9 %fusion.75 = (bf16[8,64,256]{2,1,0:T(8,128)(2,1)}, bf16[8,64,256]{2,1,0:T(8,128)(2,1)}) fusion(bf16[8,128,256]{2,1,0:T(8,128)(2,1)} %param.8), kind=kLoop, calls=%fused_computation.131 | loop fusion | bytes 1048576 | tf_op jit(solution)/shard_map/slice | solution.py:54
  1.9 10.9 %collective-permute-start.6 = (bf16[8,64,256]{2,1,0:T(8,128)(2,1)}, bf16[8,64,256]{2,1,0:T(8,128)(2,1)}, u32[]{:S(2)}, u32[]{:S(2)}) collective-permute-start(bf16[8,64,256]{2,1,0:T(8,128)(2,1)} %get-tuple-element.11), channel_id=1, source_target_pairs={{0,256},{8,264},{16,272},{24,280},{32,288},{40,296},{48,304},{56,3... | collective-permute-start | bytes 786440 | tf_op jit(solution)/shard_map/ppermute | solution.py:10
  12.8 1.9 %collective-permute-start = (f32[8,128]{1,0:T(8,128)}, f32[8,128]{1,0:T(8,128)S(1)}, u32[]{:S(2)}, u32[]{:S(2)}) collective-permute-start(f32[8,128]{1,0:T(8,128)} %param.9), channel_id=1, source_target_pairs={{0,256},{8,264},{16,272},{24,280},{32,288},{40,296},{48,304},{56,3... | collective-permute-start | bytes 12296 | tf_op jit(solution)/shard_map/ppermute | solution.py:10
  14.7 7.8 %collective-permute-start.1 = (bf16[8,64,256]{2,1,0:T(8,128)(2,1)}, bf16[8,64,256]{2,1,0:T(8,128)(2,1)}, u32[]{:S(2)}, u32[]{:S(2)}) collective-permute-start(bf16[8,64,256]{2,1,0:T(8,128)(2,1)} %get-tuple-element.12), channel_id=1, source_target_pairs={{0,256},{8,264},{16,272},{24,280},{32,288},{40,296},{48,304},{56,3... | collective-permute-start | bytes 786440 | tf_op jit(solution)/shard_map/ppermute | solution.py:10
  22.6 1.5 fusion.74
  24.8 0.9 copy-done
  28.6 0.8 slice_bitcast_fusion.2
  29.5 0.8 slice_bitcast_fusion
  30.5 1.1 fusion.17
  31.6 1.1 fusion.20
  33.0 1.6 %fusion.4 = bf16[8,64,256]{2,1,0:T(8,128)(2,1)S(1)} fusion(f32[8,64,256]{2,1,0:T(8,128)} %fusion.17, bf16[8,64,256]{2,1,0:T(8,128)(2,1)} %collective-permute-done.6, f32[8,256]{1,0:T(8,128)S(1)} %pad_maximum_fusion.1, bf16[8,128,128]{2,1,0:T(8,128)(2,1)} %get-tuple-element.24, bf16[8,128,128]{2,1,0:T(8,128)(2,1)S(1)} %fusion.62, ...), kind=kOutput, calls=%fused_computation.18 | convolution fusion | flops 71958528 | bytes 1843200 | tf_op jit(solution)/shard_map/bsi,bij->bsj/dot_general | solution.py:22
  34.7 4.4 %collective-permute-start.7 = (bf16[8,64,256]{2,1,0:T(8,128)(2,1)S(1)}, bf16[8,64,256]{2,1,0:T(8,128)(2,1)S(1)}, u32[]{:S(2)}, u32[]{:S(2)}) collective-permute-start(bf16[8,64,256]{2,1,0:T(8,128)(2,1)S(1)} %fusion.4), channel_id=1, source_target_pairs={{0,128},{8,136},{16,144},{24,152},{32,160},{40,168},{48,176},{56,1... | collective-permute-start | bytes 786440 | tf_op jit(solution)/shard_map/ppermute | solution.py:10
  40.0 1.3 fusion
  41.2 1.9 %collective-permute-start.2 = (bf16[8,64,256]{2,1,0:T(8,128)(2,1)S(1)}, bf16[8,64,256]{2,1,0:T(8,128)(2,1)S(1)}, u32[]{:S(2)}, u32[]{:S(2)}) collective-permute-start(bf16[8,64,256]{2,1,0:T(8,128)(2,1)S(1)} %fusion), channel_id=1, source_target_pairs={{0,128},{8,136},{16,144},{24,152},{32,160},{40,168},{48,176},{56,1... | collective-permute-start | bytes 786440 | tf_op jit(solution)/shard_map/ppermute | solution.py:10
  43.8 13.3 %collective-permute-done.7 = bf16[8,64,256]{2,1,0:T(8,128)(2,1)S(1)} collective-permute-done((bf16[8,64,256]{2,1,0:T(8,128)(2,1)S(1)}, bf16[8,64,256]{2,1,0:T(8,128)(2,1)S(1)}, u32[]{:S(2)}, u32[]{:S(2)}) %collective-permute-start.7) | collective-permute-done | bytes 262176 | tf_op jit(solution)/shard_map/ppermute | solution.py:10
  57.4 6.1 %collective-permute-start.8 = (bf16[8,64,256]{2,1,0:T(8,128)(2,1)S(1)}, bf16[8,64,256]{2,1,0:T(8,128)(2,1)S(1)}, u32[]{:S(2)}, u32[]{:S(2)}) collective-permute-start(bf16[8,64,256]{2,1,0:T(8,128)(2,1)S(1)} %fusion.5), channel_id=1, source_target_pairs={{0,64},{8,72},{16,80},{24,88},{32,96},{40,104},{48,112},{56,120},{... | collective-permute-start | bytes 786440 | tf_op jit(solution)/shard_map/ppermute | solution.py:10
  63.8 4.1 %collective-permute-start.3 = (bf16[8,64,256]{2,1,0:T(8,128)(2,1)S(1)}, bf16[8,64,256]{2,1,0:T(8,128)(2,1)S(1)}, u32[]{:S(2)}, u32[]{:S(2)}) collective-permute-start(bf16[8,64,256]{2,1,0:T(8,128)(2,1)S(1)} %fusion.1), channel_id=1, source_target_pairs={{0,64},{8,72},{16,80},{24,88},{32,96},{40,104},{48,112},{56,120},{... | collective-permute-start | bytes 786440 | tf_op jit(solution)/shard_map/ppermute | solution.py:10
  68.6 10.9 %collective-permute-done.8 = bf16[8,64,256]{2,1,0:T(8,128)(2,1)S(1)} collective-permute-done((bf16[8,64,256]{2,1,0:T(8,128)(2,1)S(1)}, bf16[8,64,256]{2,1,0:T(8,128)(2,1)S(1)}, u32[]{:S(2)}, u32[]{:S(2)}) %collective-permute-start.8) | collective-permute-done | bytes 262176 | tf_op jit(solution)/shard_map/ppermute | solution.py:10
  80.9 7.3 %collective-permute-start.9 = (bf16[8,64,256]{2,1,0:T(8,128)(2,1)S(1)}, bf16[8,64,256]{2,1,0:T(8,128)(2,1)S(1)}, u32[]{:S(2)}, u32[]{:S(2)}) collective-permute-start(bf16[8,64,256]{2,1,0:T(8,128)(2,1)S(1)} %convolution_convert_fusion.1), channel_id=1, source_target_pairs={{0,64},{8,72},{16,80},{24,88},{32,96},{40,104},{48,112},{56,120},{... | collective-permute-start | bytes 786440 | tf_op jit(solution)/shard_map/ppermute | solution.py:10
  88.3 5.0 %collective-permute-done.3 = bf16[8,64,256]{2,1,0:T(8,128)(2,1)S(1)} collective-permute-done((bf16[8,64,256]{2,1,0:T(8,128)(2,1)S(1)}, bf16[8,64,256]{2,1,0:T(8,128)(2,1)S(1)}, u32[]{:S(2)}, u32[]{:S(2)}) %collective-permute-start.3) | collective-permute-done | bytes 262176 | tf_op jit(solution)/shard_map/ppermute | solution.py:10
  94.7 7.0 %collective-permute-start.4 = (bf16[8,64,256]{2,1,0:T(8,128)(2,1)S(1)}, bf16[8,64,256]{2,1,0:T(8,128)(2,1)S(1)}, u32[]{:S(2)}, u32[]{:S(2)}) collective-permute-start(bf16[8,64,256]{2,1,0:T(8,128)(2,1)S(1)} %convolution_convert_fusion.4), channel_id=1, source_target_pairs={{0,64},{8,72},{16,80},{24,88},{32,96},{40,104},{48,112},{56,120},{... | collective-permute-start | bytes 786440 | tf_op jit(solution)/shard_map/ppermute | solution.py:10
  101.7 1.8 %collective-permute-done.9 = bf16[8,64,256]{2,1,0:T(8,128)(2,1)S(1)} collective-permute-done((bf16[8,64,256]{2,1,0:T(8,128)(2,1)S(1)}, bf16[8,64,256]{2,1,0:T(8,128)(2,1)S(1)}, u32[]{:S(2)}, u32[]{:S(2)}) %collective-permute-start.9) | collective-permute-done | bytes 262176 | tf_op jit(solution)/shard_map/ppermute | solution.py:10
  104.4 1.9 %collective-permute-start.10 = (bf16[8,64,256]{2,1,0:T(8,128)(2,1)S(1)}, bf16[8,64,256]{2,1,0:T(8,128)(2,1)S(1)}, u32[]{:S(2)}, u32[]{:S(2)}) collective-permute-start(bf16[8,64,256]{2,1,0:T(8,128)(2,1)S(1)} %convolution_convert_fusion), channel_id=1, source_target_pairs={{0,128},{8,136},{16,144},{24,152},{32,160},{40,168},{48,176},{56,1... | collective-permute-start | bytes 786440 | tf_op jit(solution)/shard_map/ppermute | solution.py:10
  106.3 2.7 %collective-permute-done.4 = bf16[8,64,256]{2,1,0:T(8,128)(2,1)S(1)} collective-permute-done((bf16[8,64,256]{2,1,0:T(8,128)(2,1)S(1)}, bf16[8,64,256]{2,1,0:T(8,128)(2,1)S(1)}, u32[]{:S(2)}, u32[]{:S(2)}) %collective-permute-start.4) | collective-permute-done | bytes 262176 | tf_op jit(solution)/shard_map/ppermute | solution.py:10
  109.9 2.3 %collective-permute-start.5 = (bf16[8,64,256]{2,1,0:T(8,128)(2,1)S(1)}, bf16[8,64,256]{2,1,0:T(8,128)(2,1)S(1)}, u32[]{:S(2)}, u32[]{:S(2)}) collective-permute-start(bf16[8,64,256]{2,1,0:T(8,128)(2,1)S(1)} %convolution_convert_fusion.3), channel_id=1, source_target_pairs={{0,128},{8,136},{16,144},{24,152},{32,160},{40,168},{48,176},{56,1... | collective-permute-start | bytes 786440 | tf_op jit(solution)/shard_map/ppermute | solution.py:10
  112.2 15.4 %collective-permute-done.10 = bf16[8,64,256]{2,1,0:T(8,128)(2,1)S(1)} collective-permute-done((bf16[8,64,256]{2,1,0:T(8,128)(2,1)S(1)}, bf16[8,64,256]{2,1,0:T(8,128)(2,1)S(1)}, u32[]{:S(2)}, u32[]{:S(2)}) %collective-permute-start.10) | collective-permute-done | bytes 262176 | tf_op jit(solution)/shard_map/ppermute | solution.py:10
  128.5 3.5 %collective-permute-done.5 = bf16[8,64,256]{2,1,0:T(8,128)(2,1)S(1)} collective-permute-done((bf16[8,64,256]{2,1,0:T(8,128)(2,1)S(1)}, bf16[8,64,256]{2,1,0:T(8,128)(2,1)S(1)}, u32[]{:S(2)}, u32[]{:S(2)}) %collective-permute-start.5) | collective-permute-done | bytes 262176 | tf_op jit(solution)/shard_map/ppermute | solution.py:10
  133.1 1.4 convolution_multiply_fusion
  134.5 1.4 convolution_multiply_fusion.1
  136.2 10.3 %all_to_all.5 = f32[8,1,256]{2,1,0:T(1,128)S(1)} all-to-all(f32[8,1,256]{2,1,0:T(1,128)S(1)} %reshape.21), channel_id=1, replica_groups=mesh['box'=64,'src'=8] {'src'}, dimensions={0} | all-to-all | bytes 16384 | tf_op jit(solution)/shard_map/all_to_all | solution.py:110
  147.8 4.1 %collective-permute-start.11 = (f32[8,16]{1,0:T(8,128)S(1)}, f32[8,16]{1,0:T(8,128)S(1)}, u32[]{:S(2)}, u32[]{:S(2)}) collective-permute-start(f32[8,16]{1,0:T(8,128)S(1)} %slice.177), channel_id=1, source_target_pairs={{0,256},{8,264},{16,272},{24,280},{32,288},{40,296},{48,304},{56,3... | collective-permute-start | bytes 1544 | tf_op jit(solution)/shard_map/ppermute | solution.py:10
  151.9 5.3 %collective-permute-done.11 = f32[8,16]{1,0:T(8,128)S(1)} collective-permute-done((f32[8,16]{1,0:T(8,128)S(1)}, f32[8,16]{1,0:T(8,128)S(1)}, u32[]{:S(2)}, u32[]{:S(2)}) %collective-permute-start.11) | collective-permute-done | bytes 544 | tf_op jit(solution)/shard_map/ppermute | solution.py:10
  (109 shorter events, 15.3 us)
Async XLA Ops:
  1.9 31.1 %collective-permute-start.6 = (bf16[8,64,256]{2,1,0:T(8,128)(2,1)}, bf16[8,64,256]{2,1,0:T(8,128)(2,1)}, u32[]{:S(2)}, u32[]{:S(2)}) collective-permute-start(bf16[8,64,256]{2,1,0:T(8,128)(2,1)} %get-tuple-element.11), channel_id=1, source_target_pairs={{0,256},{8,264},{16,272},{24,280},{32,288},{40,296},{48,304},{56,3... | collective-permute-start | bytes 786440 | tf_op jit(solution)/shard_map/ppermute | solution.py:10
  12.8 20.2 %collective-permute-start = (f32[8,128]{1,0:T(8,128)}, f32[8,128]{1,0:T(8,128)S(1)}, u32[]{:S(2)}, u32[]{:S(2)}) collective-permute-start(f32[8,128]{1,0:T(8,128)} %param.9), channel_id=1, source_target_pairs={{0,256},{8,264},{16,272},{24,280},{32,288},{40,296},{48,304},{56,3... | collective-permute-start | bytes 12296 | tf_op jit(solution)/shard_map/ppermute | solution.py:10
  14.7 25.2 %collective-permute-start.1 = (bf16[8,64,256]{2,1,0:T(8,128)(2,1)}, bf16[8,64,256]{2,1,0:T(8,128)(2,1)}, u32[]{:S(2)}, u32[]{:S(2)}) collective-permute-start(bf16[8,64,256]{2,1,0:T(8,128)(2,1)} %get-tuple-element.12), channel_id=1, source_target_pairs={{0,256},{8,264},{16,272},{24,280},{32,288},{40,296},{48,304},{56,3... | collective-permute-start | bytes 786440 | tf_op jit(solution)/shard_map/ppermute | solution.py:10
  24.1 1.6 %copy-start = (bf16[3,8,2,128,128]{4,3,2,1,0:T(8,128)(2,1)S(1)}, bf16[3,8,2,128,128]{4,3,2,1,0:T(8,128)(2,1)}, u32[]{:S(2)}) copy-start(bf16[3,8,2,128,128]{4,3,2,1,0:T(8,128)(2,1)} %param.11) | copy-start | bytes 4718596
  24.2 7.4 %copy-start.4 = (bf16[8,128,128]{2,1,0:T(8,128)(2,1)}, bf16[8,128,128]{2,1,0:T(8,128)(2,1)S(1)}, u32[]{:S(2)}) copy-start(bf16[8,128,128]{2,1,0:T(8,128)(2,1)S(1)} %get-tuple-element.25) | copy-start | bytes 786436
  24.2 7.4 %copy-start.6 = (bf16[8,128,128]{2,1,0:T(8,128)(2,1)}, bf16[8,128,128]{2,1,0:T(8,128)(2,1)S(1)}, u32[]{:S(2)}) copy-start(bf16[8,128,128]{2,1,0:T(8,128)(2,1)S(1)} %get-tuple-element.26) | copy-start | bytes 786436
  29.4 1.1 copy-start.2
  31.6 1.2 copy-start.1
  31.6 1.2 copy-start.17
  31.6 1.2 copy-start.18
  31.6 1.4 copy-start.19
  33.0 6.9 %copy-start.3 = (bf16[8,128,128]{2,1,0:T(8,128)(2,1)S(1)}, bf16[8,128,128]{2,1,0:T(8,128)(2,1)}, u32[]{:S(2)}) copy-start(bf16[8,128,128]{2,1,0:T(8,128)(2,1)} %get-tuple-element.24) | copy-start | bytes 786436
  33.0 6.9 %copy-start.20 = (f32[8,64,256]{2,1,0:T(8,128)S(1)}, f32[8,64,256]{2,1,0:T(8,128)}, u32[]{:S(2)}) copy-start(f32[8,64,256]{2,1,0:T(8,128)} %fusion.20) | copy-start | bytes 1572868
  34.7 8.4 %copy-start.8 = (bf16[8,128,128]{2,1,0:T(8,128)(2,1)S(1)}, bf16[8,128,128]{2,1,0:T(8,128)(2,1)}, u32[]{:S(2)}) copy-start(bf16[8,128,128]{2,1,0:T(8,128)(2,1)} %get-tuple-element.21) | copy-start | bytes 786436
  34.7 8.4 %copy-start.9 = (bf16[8,128,128]{2,1,0:T(8,128)(2,1)S(1)}, bf16[8,128,128]{2,1,0:T(8,128)(2,1)}, u32[]{:S(2)}) copy-start(bf16[8,128,128]{2,1,0:T(8,128)(2,1)} %get-tuple-element.22) | copy-start | bytes 786436
  34.7 22.4 %collective-permute-start.7 = (bf16[8,64,256]{2,1,0:T(8,128)(2,1)S(1)}, bf16[8,64,256]{2,1,0:T(8,128)(2,1)S(1)}, u32[]{:S(2)}, u32[]{:S(2)}) collective-permute-start(bf16[8,64,256]{2,1,0:T(8,128)(2,1)S(1)} %fusion.4), channel_id=1, source_target_pairs={{0,128},{8,136},{16,144},{24,152},{32,160},{40,168},{48,176},{56,1... | collective-permute-start | bytes 786440 | tf_op jit(solution)/shard_map/ppermute | solution.py:10
  41.2 22.3 %collective-permute-start.2 = (bf16[8,64,256]{2,1,0:T(8,128)(2,1)S(1)}, bf16[8,64,256]{2,1,0:T(8,128)(2,1)S(1)}, u32[]{:S(2)}, u32[]{:S(2)}) collective-permute-start(bf16[8,64,256]{2,1,0:T(8,128)(2,1)S(1)} %fusion), channel_id=1, source_target_pairs={{0,128},{8,136},{16,144},{24,152},{32,160},{40,168},{48,176},{56,1... | collective-permute-start | bytes 786440 | tf_op jit(solution)/shard_map/ppermute | solution.py:10
  43.5 13.6 %copy-start.10 = (bf16[8,128,128]{2,1,0:T(8,128)(2,1)S(1)}, bf16[8,128,128]{2,1,0:T(8,128)(2,1)}, u32[]{:S(2)}) copy-start(bf16[8,128,128]{2,1,0:T(8,128)(2,1)} %get-tuple-element.19) | copy-start | bytes 786436
  43.5 13.6 %copy-start.11 = (bf16[8,128,128]{2,1,0:T(8,128)(2,1)S(1)}, bf16[8,128,128]{2,1,0:T(8,128)(2,1)}, u32[]{:S(2)}) copy-start(bf16[8,128,128]{2,1,0:T(8,128)(2,1)} %get-tuple-element.20) | copy-start | bytes 786436
  57.4 10.6 %copy-start.12 = (bf16[8,128,128]{2,1,0:T(8,128)(2,1)S(1)}, bf16[8,128,128]{2,1,0:T(8,128)(2,1)}, u32[]{:S(2)}) copy-start(bf16[8,128,128]{2,1,0:T(8,128)(2,1)} %get-tuple-element.17) | copy-start | bytes 786436
  57.4 10.6 %copy-start.13 = (bf16[8,128,128]{2,1,0:T(8,128)(2,1)S(1)}, bf16[8,128,128]{2,1,0:T(8,128)(2,1)}, u32[]{:S(2)}) copy-start(bf16[8,128,128]{2,1,0:T(8,128)(2,1)} %get-tuple-element.18) | copy-start | bytes 786436
  57.4 22.1 %collective-permute-start.8 = (bf16[8,64,256]{2,1,0:T(8,128)(2,1)S(1)}, bf16[8,64,256]{2,1,0:T(8,128)(2,1)S(1)}, u32[]{:S(2)}, u32[]{:S(2)}) collective-permute-start(bf16[8,64,256]{2,1,0:T(8,128)(2,1)S(1)} %fusion.5), channel_id=1, source_target_pairs={{0,64},{8,72},{16,80},{24,88},{32,96},{40,104},{48,112},{56,120},{... | collective-permute-start | bytes 786440 | tf_op jit(solution)/shard_map/ppermute | solution.py:10
  63.8 29.4 %collective-permute-start.3 = (bf16[8,64,256]{2,1,0:T(8,128)(2,1)S(1)}, bf16[8,64,256]{2,1,0:T(8,128)(2,1)S(1)}, u32[]{:S(2)}, u32[]{:S(2)}) collective-permute-start(bf16[8,64,256]{2,1,0:T(8,128)(2,1)S(1)} %fusion.1), channel_id=1, source_target_pairs={{0,64},{8,72},{16,80},{24,88},{32,96},{40,104},{48,112},{56,120},{... | collective-permute-start | bytes 786440 | tf_op jit(solution)/shard_map/ppermute | solution.py:10
  68.3 11.2 %copy-start.14 = (bf16[8,128,128]{2,1,0:T(8,128)(2,1)S(1)}, bf16[8,128,128]{2,1,0:T(8,128)(2,1)}, u32[]{:S(2)}) copy-start(bf16[8,128,128]{2,1,0:T(8,128)(2,1)} %get-tuple-element.15) | copy-start | bytes 786436
  68.3 11.2 %copy-start.15 = (bf16[8,128,128]{2,1,0:T(8,128)(2,1)S(1)}, bf16[8,128,128]{2,1,0:T(8,128)(2,1)}, u32[]{:S(2)}) copy-start(bf16[8,128,128]{2,1,0:T(8,128)(2,1)} %get-tuple-element.16) | copy-start | bytes 786436
  80.9 22.6 %collective-permute-start.9 = (bf16[8,64,256]{2,1,0:T(8,128)(2,1)S(1)}, bf16[8,64,256]{2,1,0:T(8,128)(2,1)S(1)}, u32[]{:S(2)}, u32[]{:S(2)}) collective-permute-start(bf16[8,64,256]{2,1,0:T(8,128)(2,1)S(1)} %convolution_convert_fusion.1), channel_id=1, source_target_pairs={{0,64},{8,72},{16,80},{24,88},{32,96},{40,104},{48,112},{56,120},{... | collective-permute-start | bytes 786440 | tf_op jit(solution)/shard_map/ppermute | solution.py:10
  94.7 14.4 %collective-permute-start.4 = (bf16[8,64,256]{2,1,0:T(8,128)(2,1)S(1)}, bf16[8,64,256]{2,1,0:T(8,128)(2,1)S(1)}, u32[]{:S(2)}, u32[]{:S(2)}) collective-permute-start(bf16[8,64,256]{2,1,0:T(8,128)(2,1)S(1)} %convolution_convert_fusion.4), channel_id=1, source_target_pairs={{0,64},{8,72},{16,80},{24,88},{32,96},{40,104},{48,112},{56,120},{... | collective-permute-start | bytes 786440 | tf_op jit(solution)/shard_map/ppermute | solution.py:10
  104.4 23.2 %collective-permute-start.10 = (bf16[8,64,256]{2,1,0:T(8,128)(2,1)S(1)}, bf16[8,64,256]{2,1,0:T(8,128)(2,1)S(1)}, u32[]{:S(2)}, u32[]{:S(2)}) collective-permute-start(bf16[8,64,256]{2,1,0:T(8,128)(2,1)S(1)} %convolution_convert_fusion), channel_id=1, source_target_pairs={{0,128},{8,136},{16,144},{24,152},{32,160},{40,168},{48,176},{56,1... | collective-permute-start | bytes 786440 | tf_op jit(solution)/shard_map/ppermute | solution.py:10
  109.9 18.1 %copy-start.5 = (bf16[8,128,128]{2,1,0:T(8,128)(2,1)S(1)}, bf16[8,128,128]{2,1,0:T(8,128)(2,1)}, u32[]{:S(2)}) copy-start(bf16[8,128,128]{2,1,0:T(8,128)(2,1)} %copy-done.4) | copy-start | bytes 786436
  109.9 18.1 %copy-start.7 = (bf16[8,128,128]{2,1,0:T(8,128)(2,1)S(1)}, bf16[8,128,128]{2,1,0:T(8,128)(2,1)}, u32[]{:S(2)}) copy-start(bf16[8,128,128]{2,1,0:T(8,128)(2,1)} %copy-done.6) | copy-start | bytes 786436
  109.9 22.1 %collective-permute-start.5 = (bf16[8,64,256]{2,1,0:T(8,128)(2,1)S(1)}, bf16[8,64,256]{2,1,0:T(8,128)(2,1)S(1)}, u32[]{:S(2)}, u32[]{:S(2)}) collective-permute-start(bf16[8,64,256]{2,1,0:T(8,128)(2,1)S(1)} %convolution_convert_fusion.3), channel_id=1, source_target_pairs={{0,128},{8,136},{16,144},{24,152},{32,160},{40,168},{48,176},{56,1... | collective-permute-start | bytes 786440 | tf_op jit(solution)/shard_map/ppermute | solution.py:10
  147.8 9.4 %collective-permute-start.11 = (f32[8,16]{1,0:T(8,128)S(1)}, f32[8,16]{1,0:T(8,128)S(1)}, u32[]{:S(2)}, u32[]{:S(2)}) collective-permute-start(f32[8,16]{1,0:T(8,128)S(1)} %slice.177), channel_id=1, source_target_pairs={{0,256},{8,264},{16,272},{24,280},{32,288},{40,296},{48,304},{56,3... | collective-permute-start | bytes 1544 | tf_op jit(solution)/shard_map/ppermute | solution.py:10
  (1 other events, 0.7 us)

commit v2 on v0

v2 whole, which is shorter than its diff:
```python
import jax
import jax.numpy as jnp
from jax import lax
from jax.sharding import PartitionSpec as P


CHUNKS = 2


def send(x, axis, flip):
    return lax.ppermute(x, axis, [(i, i ^ flip) for i in range(lax.axis_size(axis))])


def block_form(weights):
    real_part = weights[:, 0]
    imag_part = weights[:, 1]
    upper_rows = jnp.concatenate([real_part, imag_part], axis=2)
    lower_rows = jnp.concatenate([-imag_part, real_part], axis=2)
    return jnp.concatenate([upper_rows, lower_rows], axis=1)


def forward_apply(values, block):
    return jnp.einsum("bsi,bij->bsj", values, block, preferred_element_type=jnp.float32)


def adjoint_apply(values, block):
    return jnp.einsum("bsj,bij->bsi", values, block, preferred_element_type=jnp.float32)


def stage(field, partner, own, cross):
    return (forward_apply(field, own) + forward_apply(partner, cross)).astype(jnp.bfloat16)


def image_terms(incident, adjoint):
    products = incident.astype(jnp.float32) * adjoint
    node_count = products.shape[2] // 2
    return jnp.sum(products[..., :node_count] + products[..., node_count:], axis=1)


def scaled(field, gains):
    doubled = jnp.concatenate([gains, gains], axis=1)
    return (doubled[:, None, :] * field.astype(jnp.float32)).astype(jnp.bfloat16)


def split_gains(gains):
    high = lax.reduce_precision(gains, 8, 7)
    rest = gains - high
    middle = lax.reduce_precision(rest, 8, 7)
    low = rest - middle
    rows = jnp.stack(
        [
            jnp.concatenate([high, middle], axis=1),
            jnp.concatenate([low, jnp.zeros_like(low)], axis=1),
        ],
        axis=1,
    ).astype(jnp.bfloat16)
    return jnp.pad(rows, ((0, 0), (0, 6), (0, 0)))


def join_gains(rows):
    node_count = rows.shape[2] // 2
    rows = rows.astype(jnp.float32)
    return (rows[:, 0, :node_count] + rows[:, 0, node_count:]) + rows[:, 1, :node_count]


def trace_adjoint(field, onehot, observed, scale):
    predicted = jnp.einsum("kb,bsi->ksi", onehot, field, preferred_element_type=jnp.float32)
    residual = predicted - observed.astype(jnp.float32)
    node_count = residual.shape[2] // 2
    magnitude = residual[..., :node_count] ** 2 + residual[..., node_count:] ** 2
    damping = 1.0 / jnp.sqrt(1.0 + magnitude / scale[None, :, None] ** 2)
    adj_traces = (residual * jnp.concatenate([damping, damping], axis=2)).astype(jnp.bfloat16)
    return jnp.einsum("kb,ksi->bsi", onehot, adj_traces, preferred_element_type=jnp.float32).astype(
        jnp.bfloat16
    )


def both_weights(sent_self, sent_cross, odd, flip):
    first = send(jnp.where(odd, sent_cross, sent_self), "box", flip)
    second = send(first, "src", 1)
    return jnp.where(odd, second, first), jnp.where(odd, first, second)


def body(incident, reflectivity, w_self, w_cross, receivers, observed, group_of, deltas):
    box_count, source_count, width = incident.shape
    node_count = width // 2
    box_devices = lax.axis_size("box")
    src_devices = lax.axis_size("src")
    flip0, flip1, flip2 = box_devices // 2, box_devices // 4, box_devices // 8
    box_index = lax.axis_index("box")
    odd = lax.axis_index("src") % 2 == 1
    onehot = (
        (receivers - box_index * box_count)[:, None]
        == jnp.arange(box_count, dtype=jnp.int32)[None, :]
    ).astype(jnp.bfloat16)
    group_hits = (
        group_of[:, None] == jnp.arange(deltas.shape[0], dtype=jnp.int32)[None, :]
    ).astype(jnp.float32)
    scale_src = jnp.sum(group_hits * deltas[None, :], axis=1)
    step = source_count // CHUNKS
    spans = [slice(c * step, (c + 1) * step) for c in range(CHUNKS)]

    incidents = [incident[:, span] for span in spans]
    sent = list(incidents)
    sent[0] = jnp.concatenate([sent[0], split_gains(reflectivity)], axis=1)
    came = [send(x, "box", flip0) for x in sent]
    across_gains = join_gains(came[0][:, step:])
    across_incidents = [x[:, :step] for x in came]

    far_self2, far_cross2 = both_weights(w_self[2], w_cross[2], odd, flip2)
    tag = jnp.pad(onehot[:, None, :], ((0, 0), (0, 7), (0, width - box_count)))
    far_traces = send(jnp.concatenate([observed, tag], axis=1), "box", flip2)
    far_observed = far_traces[:, :source_count]
    far_onehot = far_traces[:, source_count, :box_count]

    self0, cross0 = block_form(w_self[0]), block_form(w_cross[0])
    fields = [
        stage(scaled(x, reflectivity), scaled(p, across_gains), self0, cross0)
        for x, p in zip(incidents, across_incidents)
    ]
    nears = [send(x, "box", flip1) for x in fields]
    weights_self, weights_cross, _ = lax.optimization_barrier((w_self[1], w_cross[1], fields))
    self1, cross1 = block_form(weights_self), block_form(weights_cross)
    fields = [stage(x, p, self1, cross1) for x, p in zip(fields, nears)]
    partners = [send(x, "box", flip2) for x in fields]
    weights_self, weights_cross, _ = lax.optimization_barrier((w_self[2], w_cross[2], fields))
    self2, cross2 = block_form(weights_self), block_form(weights_cross)
    far_self2, far_cross2 = block_form(far_self2), block_form(far_cross2)

    adjoints = []
    received = []
    for c, (span, field, partner) in enumerate(zip(spans, fields, partners)):
        if c:
            partner, _ = lax.optimization_barrier((partner, outgoing))
        top = stage(field, partner, self2, cross2)
        far_top = stage(partner, field, far_self2, far_cross2)
        own = trace_adjoint(top, onehot, observed[:, span], scale_src[span])
        far = trace_adjoint(far_top, far_onehot, far_observed[:, span], scale_src[span])
        adjoint = adjoint_apply(own, self2) + adjoint_apply(far, far_cross2)
        adjoints.append(adjoint.astype(jnp.bfloat16))
        outgoing = adjoint_apply(adjoints[-1], cross1).astype(jnp.bfloat16)
        received.append(send(outgoing, "box", flip1))
    adjoints = [
        (adjoint_apply(x, self1) + r.astype(jnp.float32)).astype(jnp.bfloat16)
        for x, r in zip(adjoints, received)
    ]
    own = across = 0.0
    for x, p, a in zip(incidents, across_incidents, adjoints):
        own += image_terms(x, adjoint_apply(a, self0))
        across += image_terms(p, adjoint_apply(a, cross0))

    share = node_count // src_devices
    upper = (box_index & flip0) != 0
    both = jnp.where(upper, jnp.stack([across, own]), jnp.stack([own, across]))
    pieces = both.reshape(2, box_count, src_devices, share).transpose(0, 2, 1, 3)
    pieces = pieces.reshape(2 * src_devices, box_count, share)
    groups = [
        [b * src_devices + s for b in (g, g + flip0) for s in range(src_devices)]
        for g in range(flip0)
    ]
    gathered = lax.all_to_all(pieces, ("box", "src"), 0, 0, axis_index_groups=groups)
    return jnp.sum(gathered, axis=0)


def solution(mesh):
    in_specs = (
        P("box", "src", None),
        P("box", None),
        P(None, "box", None, None, None),
        P(None, "box", None, None, None),
        P("box"),
        P("box", "src", None),
        P("src"),
        P(),
    )
    out_specs = P("box", "src")

    return jax.shard_map(body, mesh=mesh, in_specs=in_specs, out_specs=out_specs, check_vma=False)
```

time: 216 us -> 155 us (0.72)
  the two profiles are of different devices: /device:TPU:104 before, /device:TPU:40 now
where the time goes in v2:
time: 155 us; the launch traced here: 154 us
  starting transfers between devices  49.3 us (32%)
  waiting for transfers between devices  47.7 us (31%)
  matrix products  20.9 us (13%)
  blocking collectives  18.9 us (12%)
  local copies, waits for them, and re-layouts  8.89 us (6%)
  other arithmetic  7.48 us (5%)
    ppermute x11, starting transfers between devices, send(): lax.ppermute(x, axis, [(i, i ^ flip) for i in range(lax.axis_size(axis))])  49.3 us
    ppermute x11, waiting for transfers between devices, send(): lax.ppermute(x, axis, [(i, i ^ flip) for i in range(lax.axis_size(axis))])  47.7 us
    all_to_all x1, blocking collectives, body(): lax.all_to_all(pieces, ('box', 'src'), 0, 0, axis_index_groups=groups)  18.9 us
    dot_general x16, matrix products, forward_apply(): jnp.einsum('bsi,bij->bsj', values, block, preferred_element_type=jnp.floa...  8.37 us
    dot_general x12, matrix products, adjoint_apply(): jnp.einsum('bsj,bij->bsi', values, block, preferred_element_type=jnp.floa...  7.22 us
  transfers between devices with their start and end apart: 11, of which 4 were waited for; matrix products, arithmetic and copies ran while one was open for 18% of the time, Pallas kernels for 0%

profile of v2, /device:TPU:40, one launch (start us, length us, event | category | flops | bytes accessed | tf_op | source)
XLA Modules:
  0.0 154.0 jit_solution(3217845948734003715)
XLA Ops:
  0.8 1.8 %fusion.105 = (bf16[8,64,256]{2,1,0:T(8,128)(2,1)}, bf16[8,64,256]{2,1,0:T(8,128)(2,1)S(1)}) fusion(bf16[8,128,256]{2,1,0:T(8,128)(2,1)} %param.8), kind=kLoop, calls=%fused_computation.196 | loop fusion | bytes 1048576 | tf_op jit(solution)/shard_map/slice | solution.py:103
  2.7 10.9 %collective-permute-start = (bf16[8,72,256]{2,1,0:T(8,128)(2,1)S(1)}, bf16[8,72,256]{2,1,0:T(8,128)(2,1)}, u32[]{:S(2)}, u32[]{:S(2)}) collective-permute-start(bf16[8,72,256]{2,1,0:T(8,128)(2,1)S(1)} %pad_maximum_fusion.1), channel_id=1, source_target_pairs={{0,256},{8,264},{16,272},{24,280},{32,288},{40,296},{48,304},{56,3... | collective-permute-start | bytes 884744 | tf_op jit(solution)/shard_map/ppermute | solution.py:11
  13.6 1.9 %collective-permute-start.1 = (bf16[8,64,256]{2,1,0:T(8,128)(2,1)}, bf16[8,64,256]{2,1,0:T(8,128)(2,1)}, u32[]{:S(2)}, u32[]{:S(2)}) collective-permute-start(bf16[8,64,256]{2,1,0:T(8,128)(2,1)} %get-tuple-element.35), channel_id=1, source_target_pairs={{0,256},{8,264},{16,272},{24,280},{32,288},{40,296},{48,304},{56,3... | collective-permute-start | bytes 786440 | tf_op jit(solution)/shard_map/ppermute | solution.py:11
  15.9 0.9 pad_maximum_fusion
  16.8 2.9 %collective-permute-start.5 = (bf16[8,136,256]{2,0,1:T(8,128)(2,1)}, bf16[8,136,256]{2,0,1:T(8,128)(2,1)}, u32[]{:S(2)}, u32[]{:S(2)}) collective-permute-start(bf16[8,136,256]{2,0,1:T(8,128)(2,1)} %pad_maximum_fusion), channel_id=1, source_target_pairs={{0,64},{8,72},{16,80},{24,88},{32,96},{40,104},{48,112},{56,120},{... | collective-permute-start | bytes 1671176 | tf_op jit(solution)/shard_map/ppermute | solution.py:11
  19.7 1.6 %fusion.104 = (bf16[1,8,2,128,128]{4,3,2,1,0:T(8,128)(2,1)S(1)}, bf16[1,8,2,128,128]{4,3,2,1,0:T(8,128)(2,1)S(1)}, bf16[1,8,2,128,128]{4,3,2,1,0:T(8,128)(2,1)S(1)}) fusion(bf16[3,8,2,128,128]{4,3,2,1,0:T(8,128)(2,1)} %param.10), kind=kLoop, calls=%fused_computation.195 | loop fusion | bytes 3145728 | tf_op jit(solution)/shard_map/slice | solution.py:126
  21.6 0.9 fusion.103
  23.4 6.8 %collective-permute-start.6 = (bf16[8,2,128,128]{3,2,0,1:T(8,128)(2,1)}, bf16[8,2,128,128]{3,2,0,1:T(8,128)(2,1)}, u32[]{:S(2)}, u32[]{:S(2)}) collective-permute-start(bf16[8,2,128,128]{3,2,0,1:T(8,128)(2,1)} %broadcast_select_fusion.2), channel_id=1, source_target_pairs={{0,64},{8,72},{16,80},{24,88},{32,96},{40,104},{48,112},{56,120},{... | collective-permute-start | bytes 1572872 | tf_op jit(solution)/shard_map/ppermute | solution.py:11
  32.0 1.1 fusion.25
  33.2 1.1 fusion.23
  35.1 1.2 copy_bitcast_fusion.2
  37.1 1.3 fusion
  38.5 1.3 fusion.1
  39.8 4.3 %collective-permute-start.2 = (bf16[8,64,256]{2,1,0:T(8,128)(2,1)S(1)}, bf16[8,64,256]{2,1,0:T(8,128)(2,1)S(1)}, u32[]{:S(2)}, u32[]{:S(2)}) collective-permute-start(bf16[8,64,256]{2,1,0:T(8,128)(2,1)S(1)} %fusion), channel_id=1, source_target_pairs={{0,128},{8,136},{16,144},{24,152},{32,160},{40,168},{48,176},{56,1... | collective-permute-start | bytes 786440 | tf_op jit(solution)/shard_map/ppermute | solution.py:11
  44.7 2.5 %collective-permute-start.3 = (bf16[8,64,256]{2,1,0:T(8,128)(2,1)S(1)}, bf16[8,64,256]{2,1,0:T(8,128)(2,1)S(1)}, u32[]{:S(2)}, u32[]{:S(2)}) collective-permute-start(bf16[8,64,256]{2,1,0:T(8,128)(2,1)S(1)} %fusion.1), channel_id=1, source_target_pairs={{0,128},{8,136},{16,144},{24,152},{32,160},{40,168},{48,176},{56,1... | collective-permute-start | bytes 786440 | tf_op jit(solution)/shard_map/ppermute | solution.py:11
  47.3 24.1 %collective-permute-done.6 = bf16[8,2,128,128]{3,2,0,1:T(8,128)(2,1)} collective-permute-done((bf16[8,2,128,128]{3,2,0,1:T(8,128)(2,1)}, bf16[8,2,128,128]{3,2,0,1:T(8,128)(2,1)}, u32[]{:S(2)}, u32[]{:S(2)}) %collective-permute-start.6) | collective-permute-done | bytes 524320 | tf_op jit(solution)/shard_map/ppermute | solution.py:11
  71.4 3.4 %collective-permute-start.7 = (bf16[8,2,128,128]{3,2,0,1:T(8,128)(2,1)}, bf16[8,2,128,128]{3,2,0,1:T(8,128)(2,1)S(1)}, u32[]{:S(2)}, u32[]{:S(2)}) collective-permute-start(bf16[8,2,128,128]{3,2,0,1:T(8,128)(2,1)} %collective-permute-done.6), channel_id=1, source_target_pairs={{0,1},{1,0},{2,3},{3,2},{4,5},{5,4},{6,7},{7,6},{8,9},{9,8},{10,11... | collective-permute-start | bytes 1572872 | tf_op jit(solution)/shard_map/ppermute | solution.py:11
  75.5 2.9 %collective-permute-start.4 = (bf16[8,64,256]{2,1,0:T(8,128)(2,1)S(1)}, bf16[8,64,256]{2,1,0:T(8,128)(2,1)S(1)}, u32[]{:S(2)}, u32[]{:S(2)}) collective-permute-start(bf16[8,64,256]{2,1,0:T(8,128)(2,1)S(1)} %fusion.2), channel_id=1, source_target_pairs={{0,64},{8,72},{16,80},{24,88},{32,96},{40,104},{48,112},{56,120},{... | collective-permute-start | bytes 786440 | tf_op jit(solution)/shard_map/ppermute | solution.py:11
  79.1 6.9 %collective-permute-start.9 = (bf16[8,64,256]{2,1,0:T(8,128)(2,1)S(1)}, bf16[8,64,256]{2,1,0:T(8,128)(2,1)S(1)}, u32[]{:S(2)}, u32[]{:S(2)}) collective-permute-start(bf16[8,64,256]{2,1,0:T(8,128)(2,1)S(1)} %fusion.3), channel_id=1, source_target_pairs={{0,64},{8,72},{16,80},{24,88},{32,96},{40,104},{48,112},{56,120},{... | collective-permute-start | bytes 786440 | tf_op jit(solution)/shard_map/ppermute | solution.py:11
  86.0 13.0 %collective-permute-done.4 = bf16[8,64,256]{2,1,0:T(8,128)(2,1)S(1)} collective-permute-done((bf16[8,64,256]{2,1,0:T(8,128)(2,1)S(1)}, bf16[8,64,256]{2,1,0:T(8,128)(2,1)S(1)}, u32[]{:S(2)}, u32[]{:S(2)}) %collective-permute-start.4) | collective-permute-done | bytes 262176 | tf_op jit(solution)/shard_map/ppermute | solution.py:11
  99.6 1.1 broadcast_select_fusion.1
  101.5 1.2 convolution_subtract_fusion.1
  103.6 1.0 convolution_convert_fusion.4
  105.9 4.3 %collective-permute-start.8 = (bf16[8,64,256]{2,1,0:T(8,128)(2,1)S(1)}, bf16[8,64,256]{2,1,0:T(8,128)(2,1)S(1)}, u32[]{:S(2)}, u32[]{:S(2)}) collective-permute-start(bf16[8,64,256]{2,1,0:T(8,128)(2,1)S(1)} %convolution_convert_fusion.3), channel_id=1, source_target_pairs={{0,128},{8,136},{16,144},{24,152},{32,160},{40,168},{48,176},{56,1... | collective-permute-start | bytes 786440 | tf_op jit(solution)/shard_map/ppermute | solution.py:11
  111.4 1.2 convolution_subtract_fusion
  113.4 1.0 convolution_convert_fusion.1
  115.3 2.6 %collective-permute-start.10 = (bf16[8,64,256]{2,1,0:T(8,128)(2,1)S(1)}, bf16[8,64,256]{2,1,0:T(8,128)(2,1)S(1)}, u32[]{:S(2)}, u32[]{:S(2)}) collective-permute-start(bf16[8,64,256]{2,1,0:T(8,128)(2,1)S(1)} %convolution_convert_fusion), channel_id=1, source_target_pairs={{0,128},{8,136},{16,144},{24,152},{32,160},{40,168},{48,176},{56,1... | collective-permute-start | bytes 786440 | tf_op jit(solution)/shard_map/ppermute | solution.py:11
  118.3 7.4 %collective-permute-done.8 = bf16[8,64,256]{2,1,0:T(8,128)(2,1)S(1)} collective-permute-done((bf16[8,64,256]{2,1,0:T(8,128)(2,1)S(1)}, bf16[8,64,256]{2,1,0:T(8,128)(2,1)S(1)}, u32[]{:S(2)}, u32[]{:S(2)}) %collective-permute-start.8) | collective-permute-done | bytes 262176 | tf_op jit(solution)/shard_map/ppermute | solution.py:11
  126.3 3.2 %collective-permute-done.10 = bf16[8,64,256]{2,1,0:T(8,128)(2,1)S(1)} collective-permute-done((bf16[8,64,256]{2,1,0:T(8,128)(2,1)S(1)}, bf16[8,64,256]{2,1,0:T(8,128)(2,1)S(1)}, u32[]{:S(2)}, u32[]{:S(2)}) %collective-permute-start.10) | collective-permute-done | bytes 262176 | tf_op jit(solution)/shard_map/ppermute | solution.py:11
  130.1 1.4 convolution_multiply_fusion.3
  131.5 1.4 convolution_multiply_fusion.2
  133.2 18.9 %all_to_all.5 = f32[16,1,128]{2,1,0:T(1,128)S(1)} all-to-all(f32[16,1,128]{2,1,0:T(1,128)S(1)} %reshape.90), channel_id=1, replica_groups={{0,1,2,3,4,5,6,7,256,257,258,259,260,261,262,263},{8,9,10,11,12,13,14,1..., dimensions={0} | all-to-all | bytes 16384 | tf_op jit(solution)/shard_map/all_to_all | solution.py:161
  (128 shorter events, 17.9 us)
Async XLA Ops:
  0.0 15.5 %copy-start.1 = (bf16[8,128,256]{2,1,0:T(8,128)(2,1)S(1)}, bf16[8,128,256]{2,1,0:T(8,128)(2,1)}, u32[]{:S(2)}) copy-start(bf16[8,128,256]{2,1,0:T(8,128)(2,1)} %param.13) | copy-start | bytes 1572868
  0.0 15.8 %copy-start.14 = (s32[8]{0:T(128)S(1)}, s32[8]{0:T(128)}, u32[]{:S(2)}) copy-start(s32[8]{0:T(128)} %param.12) | copy-start | bytes 100
  2.7 33.7 %collective-permute-start = (bf16[8,72,256]{2,1,0:T(8,128)(2,1)S(1)}, bf16[8,72,256]{2,1,0:T(8,128)(2,1)}, u32[]{:S(2)}, u32[]{:S(2)}) collective-permute-start(bf16[8,72,256]{2,1,0:T(8,128)(2,1)S(1)} %pad_maximum_fusion.1), channel_id=1, source_target_pairs={{0,256},{8,264},{16,272},{24,280},{32,288},{40,296},{48,304},{56,3... | collective-permute-start | bytes 884744 | tf_op jit(solution)/shard_map/ppermute | solution.py:11
  13.6 24.9 %collective-permute-start.1 = (bf16[8,64,256]{2,1,0:T(8,128)(2,1)}, bf16[8,64,256]{2,1,0:T(8,128)(2,1)}, u32[]{:S(2)}, u32[]{:S(2)}) collective-permute-start(bf16[8,64,256]{2,1,0:T(8,128)(2,1)} %get-tuple-element.35), channel_id=1, source_target_pairs={{0,256},{8,264},{16,272},{24,280},{32,288},{40,296},{48,304},{56,3... | collective-permute-start | bytes 786440 | tf_op jit(solution)/shard_map/ppermute | solution.py:11
  16.8 84.7 %collective-permute-start.5 = (bf16[8,136,256]{2,0,1:T(8,128)(2,1)}, bf16[8,136,256]{2,0,1:T(8,128)(2,1)}, u32[]{:S(2)}, u32[]{:S(2)}) collective-permute-start(bf16[8,136,256]{2,0,1:T(8,128)(2,1)} %pad_maximum_fusion), channel_id=1, source_target_pairs={{0,64},{8,72},{16,80},{24,88},{32,96},{40,104},{48,112},{56,120},{... | collective-permute-start | bytes 1671176 | tf_op jit(solution)/shard_map/ppermute | solution.py:11
  19.7 1.9 %copy-start = (bf16[3,8,2,128,128]{4,3,2,1,0:T(8,128)(2,1)S(1)}, bf16[3,8,2,128,128]{4,3,2,1,0:T(8,128)(2,1)}, u32[]{:S(2)}) copy-start(bf16[3,8,2,128,128]{4,3,2,1,0:T(8,128)(2,1)} %param.11) | copy-start | bytes 4718596
  22.5 7.7 %copy-start.13 = (f32[8,128]{1,0:T(8,128)S(1)}, f32[8,128]{1,0:T(8,128)}, u32[]{:S(2)}) copy-start(f32[8,128]{1,0:T(8,128)} %param.9) | copy-start | bytes 12292
  23.4 48.0 %collective-permute-start.6 = (bf16[8,2,128,128]{3,2,0,1:T(8,128)(2,1)}, bf16[8,2,128,128]{3,2,0,1:T(8,128)(2,1)}, u32[]{:S(2)}, u32[]{:S(2)}) collective-permute-start(bf16[8,2,128,128]{3,2,0,1:T(8,128)(2,1)} %broadcast_select_fusion.2), channel_id=1, source_target_pairs={{0,64},{8,72},{16,80},{24,88},{32,96},{40,104},{48,112},{56,120},{... | collective-permute-start | bytes 1572872 | tf_op jit(solution)/shard_map/ppermute | solution.py:11
  30.3 2.8 %copy-start.9 = (bf16[8,128,128]{2,1,0:T(8,128)(2,1)}, bf16[8,128,128]{2,1,0:T(8,128)(2,1)S(1)}, u32[]{:S(2)}) copy-start(bf16[8,128,128]{2,1,0:T(8,128)(2,1)S(1)} %get-tuple-element.39) | copy-start | bytes 786436
  30.3 2.8 %copy-start.11 = (bf16[8,128,128]{2,1,0:T(8,128)(2,1)}, bf16[8,128,128]{2,1,0:T(8,128)(2,1)S(1)}, u32[]{:S(2)}) copy-start(bf16[8,128,128]{2,1,0:T(8,128)(2,1)S(1)} %get-tuple-element.40) | copy-start | bytes 786436
  30.4 1.7 %copy-start.2 = (bf16[8,128,256]{2,1,0:T(8,128)(2,1)S(1)}, bf16[8,128,256]{2,1,0:T(8,128)(2,1)}, u32[]{:S(2)}) copy-start(bf16[8,128,256]{2,1,0:T(8,128)(2,1)} %param.8) | copy-start | bytes 1572868
  30.4 2.7 %copy-start.5 = (bf16[8,128,128]{2,1,0:T(8,128)(2,1)}, bf16[8,128,128]{2,1,0:T(8,128)(2,1)S(1)}, u32[]{:S(2)}) copy-start(bf16[8,128,128]{2,1,0:T(8,128)(2,1)S(1)} %fusion.89) | copy-start | bytes 786436
  34.3 0.7 copy-start.15
  34.3 0.7 copy-start.16
  34.9 2.2 %copy-start.4 = (bf16[8,128,128]{2,1,0:T(8,128)(2,1)S(1)}, bf16[8,128,128]{2,1,0:T(8,128)(2,1)}, u32[]{:S(2)}) copy-start(bf16[8,128,128]{2,1,0:T(8,128)(2,1)} %fusion.90) | copy-start | bytes 786436
  34.9 2.2 %copy-start.7 = (bf16[8,128,128]{2,1,0:T(8,128)(2,1)S(1)}, bf16[8,128,128]{2,1,0:T(8,128)(2,1)}, u32[]{:S(2)}) copy-start(bf16[8,128,128]{2,1,0:T(8,128)(2,1)} %get-tuple-element.37) | copy-start | bytes 786436
  34.9 2.2 %copy-start.8 = (bf16[8,128,128]{2,1,0:T(8,128)(2,1)S(1)}, bf16[8,128,128]{2,1,0:T(8,128)(2,1)}, u32[]{:S(2)}) copy-start(bf16[8,128,128]{2,1,0:T(8,128)(2,1)} %get-tuple-element.38) | copy-start | bytes 786436
  35.1 2.0 %copy-start.20 = (f32[8,64,256]{2,1,0:T(8,128)S(1)}, f32[8,64,256]{2,1,0:T(8,128)}, u32[]{:S(2)}) copy-start(f32[8,64,256]{2,1,0:T(8,128)} %fusion.25) | copy-start | bytes 1572868
  37.1 1.3 copy-start.19
  39.8 34.9 %collective-permute-start.2 = (bf16[8,64,256]{2,1,0:T(8,128)(2,1)S(1)}, bf16[8,64,256]{2,1,0:T(8,128)(2,1)S(1)}, u32[]{:S(2)}, u32[]{:S(2)}) collective-permute-start(bf16[8,64,256]{2,1,0:T(8,128)(2,1)S(1)} %fusion), channel_id=1, source_target_pairs={{0,128},{8,136},{16,144},{24,152},{32,160},{40,168},{48,176},{56,1... | collective-permute-start | bytes 786440 | tf_op jit(solution)/shard_map/ppermute | solution.py:11
  44.7 30.4 %collective-permute-start.3 = (bf16[8,64,256]{2,1,0:T(8,128)(2,1)S(1)}, bf16[8,64,256]{2,1,0:T(8,128)(2,1)S(1)}, u32[]{:S(2)}, u32[]{:S(2)}) collective-permute-start(bf16[8,64,256]{2,1,0:T(8,128)(2,1)S(1)} %fusion.1), channel_id=1, source_target_pairs={{0,128},{8,136},{16,144},{24,152},{32,160},{40,168},{48,176},{56,1... | collective-permute-start | bytes 786440 | tf_op jit(solution)/shard_map/ppermute | solution.py:11
  71.4 28.2 %collective-permute-start.7 = (bf16[8,2,128,128]{3,2,0,1:T(8,128)(2,1)}, bf16[8,2,128,128]{3,2,0,1:T(8,128)(2,1)S(1)}, u32[]{:S(2)}, u32[]{:S(2)}) collective-permute-start(bf16[8,2,128,128]{3,2,0,1:T(8,128)(2,1)} %collective-permute-done.6), channel_id=1, source_target_pairs={{0,1},{1,0},{2,3},{3,2},{4,5},{5,4},{6,7},{7,6},{8,9},{9,8},{10,11... | collective-permute-start | bytes 1572872 | tf_op jit(solution)/shard_map/ppermute | solution.py:11
  75.5 23.4 %collective-permute-start.4 = (bf16[8,64,256]{2,1,0:T(8,128)(2,1)S(1)}, bf16[8,64,256]{2,1,0:T(8,128)(2,1)S(1)}, u32[]{:S(2)}, u32[]{:S(2)}) collective-permute-start(bf16[8,64,256]{2,1,0:T(8,128)(2,1)S(1)} %fusion.2), channel_id=1, source_target_pairs={{0,64},{8,72},{16,80},{24,88},{32,96},{40,104},{48,112},{56,120},{... | collective-permute-start | bytes 786440 | tf_op jit(solution)/shard_map/ppermute | solution.py:11
  79.1 31.3 %collective-permute-start.9 = (bf16[8,64,256]{2,1,0:T(8,128)(2,1)S(1)}, bf16[8,64,256]{2,1,0:T(8,128)(2,1)S(1)}, u32[]{:S(2)}, u32[]{:S(2)}) collective-permute-start(bf16[8,64,256]{2,1,0:T(8,128)(2,1)S(1)} %fusion.3), channel_id=1, source_target_pairs={{0,64},{8,72},{16,80},{24,88},{32,96},{40,104},{48,112},{56,120},{... | collective-permute-start | bytes 786440 | tf_op jit(solution)/shard_map/ppermute | solution.py:11
  105.4 20.4 %copy-start.17 = (f32[8,64,256]{2,1,0:T(8,128)}, f32[8,64,256]{2,1,0:T(8,128)S(1)}, u32[]{:S(2)}) copy-start(f32[8,64,256]{2,1,0:T(8,128)S(1)} %fusion.100) | copy-start | bytes 1572868
  105.9 19.9 %collective-permute-start.8 = (bf16[8,64,256]{2,1,0:T(8,128)(2,1)S(1)}, bf16[8,64,256]{2,1,0:T(8,128)(2,1)S(1)}, u32[]{:S(2)}, u32[]{:S(2)}) collective-permute-start(bf16[8,64,256]{2,1,0:T(8,128)(2,1)S(1)} %convolution_convert_fusion.3), channel_id=1, source_target_pairs={{0,128},{8,136},{16,144},{24,152},{32,160},{40,168},{48,176},{56,1... | collective-permute-start | bytes 786440 | tf_op jit(solution)/shard_map/ppermute | solution.py:11
  115.3 10.5 %copy-start.3 = (bf16[8,128,256]{2,1,0:T(8,128)(2,1)S(1)}, bf16[8,128,256]{2,1,0:T(8,128)(2,1)}, u32[]{:S(2)}) copy-start(bf16[8,128,256]{2,1,0:T(8,128)(2,1)} %param.8) | copy-start | bytes 1572868
  115.3 10.5 %copy-start.6 = (bf16[8,128,128]{2,1,0:T(8,128)(2,1)S(1)}, bf16[8,128,128]{2,1,0:T(8,128)(2,1)}, u32[]{:S(2)}) copy-start(bf16[8,128,128]{2,1,0:T(8,128)(2,1)} %copy-done.5) | copy-start | bytes 786436
  115.3 10.5 %copy-start.10 = (bf16[8,128,128]{2,1,0:T(8,128)(2,1)S(1)}, bf16[8,128,128]{2,1,0:T(8,128)(2,1)}, u32[]{:S(2)}) copy-start(bf16[8,128,128]{2,1,0:T(8,128)(2,1)} %copy-done.9) | copy-start | bytes 786436
  115.3 10.5 %copy-start.12 = (bf16[8,128,128]{2,1,0:T(8,128)(2,1)S(1)}, bf16[8,128,128]{2,1,0:T(8,128)(2,1)}, u32[]{:S(2)}) copy-start(bf16[8,128,128]{2,1,0:T(8,128)(2,1)} %copy-done.11) | copy-start | bytes 786436
  115.3 14.2 %collective-permute-start.10 = (bf16[8,64,256]{2,1,0:T(8,128)(2,1)S(1)}, bf16[8,64,256]{2,1,0:T(8,128)(2,1)S(1)}, u32[]{:S(2)}, u32[]{:S(2)}) collective-permute-start(bf16[8,64,256]{2,1,0:T(8,128)(2,1)S(1)} %convolution_convert_fusion), channel_id=1, source_target_pairs={{0,128},{8,136},{16,144},{24,152},{32,160},{40,168},{48,176},{56,1... | collective-permute-start | bytes 786440 | tf_op jit(solution)/shard_map/ppermute | solution.py:11
  126.3 3.8 %copy-start.18 = (f32[8,64,256]{2,1,0:T(8,128)S(1)}, f32[8,64,256]{2,1,0:T(8,128)}, u32[]{:S(2)}) copy-start(f32[8,64,256]{2,1,0:T(8,128)} %copy-done.17) | copy-start | bytes 1572868

commit v3 on v2

--- a/solution.py
+++ b/solution.py
@@ -4,19 +4,21 @@
 from jax.sharding import PartitionSpec as P
 
 
-CHUNKS = 2
+CHUNKS = (64, 64)
 
 
 def send(x, axis, flip):
     return lax.ppermute(x, axis, [(i, i ^ flip) for i in range(lax.axis_size(axis))])
 
 
-def block_form(weights):
-    real_part = weights[:, 0]
-    imag_part = weights[:, 1]
+def join_parts(real_part, imag_part):
     upper_rows = jnp.concatenate([real_part, imag_part], axis=2)
     lower_rows = jnp.concatenate([-imag_part, real_part], axis=2)
     return jnp.concatenate([upper_rows, lower_rows], axis=1)
+
+
+def block_form(weights):
+    return join_parts(weights[:, 0], weights[:, 1])
 
 
 def forward_apply(values, block):
@@ -28,7 +30,8 @@
 
 
 def stage(field, partner, own, cross):
-    return (forward_apply(field, own) + forward_apply(partner, cross)).astype(jnp.bfloat16)
+    kept = forward_apply(field, own)
+    return (kept + forward_apply(partner, cross)).astype(jnp.bfloat16)
 
 
 def image_terms(incident, adjoint):
@@ -75,10 +78,9 @@
     )
 
 
-def both_weights(sent_self, sent_cross, odd, flip):
-    first = send(jnp.where(odd, sent_cross, sent_self), "box", flip)
-    second = send(first, "src", 1)
-    return jnp.where(odd, second, first), jnp.where(odd, first, second)
+def pick(parts, index):
+    low, high = (index & 1) != 0, (index & 2) != 0
+    return jnp.where(high, jnp.where(low, parts[3], parts[2]), jnp.where(low, parts[1], parts[0]))
 
 
 def body(incident, reflectivity, w_self, w_cross, receivers, observed, group_of, deltas):
@@ -88,7 +90,7 @@
     src_devices = lax.axis_size("src")
     flip0, flip1, flip2 = box_devices // 2, box_devices // 4, box_devices // 8
     box_index = lax.axis_index("box")
-    odd = lax.axis_index("src") % 2 == 1
+    quarter = lax.axis_index("src") % 4
     onehot = (
         (receivers - box_index * box_count)[:, None]
         == jnp.arange(box_count, dtype=jnp.int32)[None, :]
@@ -97,21 +99,26 @@
         group_of[:, None] == jnp.arange(deltas.shape[0], dtype=jnp.int32)[None, :]
     ).astype(jnp.float32)
     scale_src = jnp.sum(group_hits * deltas[None, :], axis=1)
-    step = source_count // CHUNKS
-    spans = [slice(c * step, (c + 1) * step) for c in range(CHUNKS)]
+    ends = [sum(CHUNKS[: c + 1]) for c in range(len(CHUNKS))]
+    assert ends[-1] == source_count
+    spans = [slice(end - size, end) for end, size in zip(ends, CHUNKS)]
 
     incidents = [incident[:, span] for span in spans]
     sent = list(incidents)
     sent[0] = jnp.concatenate([sent[0], split_gains(reflectivity)], axis=1)
     came = [send(x, "box", flip0) for x in sent]
-    across_gains = join_gains(came[0][:, step:])
-    across_incidents = [x[:, :step] for x in came]
+    across_gains = join_gains(came[0][:, CHUNKS[0] :])
+    across_incidents = [x[:, :size] for x, size in zip(came, CHUNKS)]
 
-    far_self2, far_cross2 = both_weights(w_self[2], w_cross[2], odd, flip2)
     tag = jnp.pad(onehot[:, None, :], ((0, 0), (0, 7), (0, width - box_count)))
+    parts = [w[2, :, k] for w in (w_self, w_cross) for k in range(2)]
+    parts = [send(pick(parts, quarter), "box", flip2)]
+    parts += [send(parts[0], "src", k) for k in (1, 2, 3)]
     far_traces = send(jnp.concatenate([observed, tag], axis=1), "box", flip2)
     far_observed = far_traces[:, :source_count]
     far_onehot = far_traces[:, source_count, :box_count]
+    parts = [pick(parts, quarter ^ k) for k in range(4)]
+    far_self2, far_cross2 = join_parts(*parts[:2]), join_parts(*parts[2:])
 
     self0, cross0 = block_form(w_self[0]), block_form(w_cross[0])
     fields = [
@@ -119,13 +126,15 @@
         for x, p in zip(incidents, across_incidents)
     ]
     nears = [send(x, "box", flip1) for x in fields]
-    weights_self, weights_cross, _ = lax.optimization_barrier((w_self[1], w_cross[1], fields))
+    weights_self, weights_cross, _ = lax.optimization_barrier((w_self[1], w_cross[1], fields[0]))
     self1, cross1 = block_form(weights_self), block_form(weights_cross)
     fields = [stage(x, p, self1, cross1) for x, p in zip(fields, nears)]
+    across_incidents, far_observed, _ = lax.optimization_barrier(
+        (across_incidents, [far_observed[:, span] for span in spans], fields[0])
+    )
     partners = [send(x, "box", flip2) for x in fields]
-    weights_self, weights_cross, _ = lax.optimization_barrier((w_self[2], w_cross[2], fields))
+    weights_self, weights_cross, _ = lax.optimization_barrier((w_self[2], w_cross[2], fields[0]))
     self2, cross2 = block_form(weights_self), block_form(weights_cross)
-    far_self2, far_cross2 = block_form(far_self2), block_form(far_cross2)
 
     adjoints = []
     received = []
@@ -135,7 +144,7 @@
         top = stage(field, partner, self2, cross2)
         far_top = stage(partner, field, far_self2, far_cross2)
         own = trace_adjoint(top, onehot, observed[:, span], scale_src[span])
-        far = trace_adjoint(far_top, far_onehot, far_observed[:, span], scale_src[span])
+        far = trace_adjoint(far_top, far_onehot, far_observed[c], scale_src[span])
         adjoint = adjoint_apply(own, self2) + adjoint_apply(far, far_cross2)
         adjoints.append(adjoint.astype(jnp.bfloat16))
         outgoing = adjoint_apply(adjoints[-1], cross1).astype(jnp.bfloat16)

time: 155 us -> 164 us (1.058)
  the two profiles are of different devices: /device:TPU:40 before, /device:TPU:56 now
where the time goes in v3:
time: 164 us; the launch traced here: 163 us
  waiting for transfers between devices  56.4 us (34%)
  starting transfers between devices  53.2 us (32%)
  blocking collectives  18.5 us (11%)
  matrix products  18.4 us (11%)
  local copies, waits for them, and re-layouts  8.29 us (5%)
  other arithmetic  7.47 us (5%)
    ppermute x13, waiting for transfers between devices, send(): lax.ppermute(x, axis, [(i, i ^ flip) for i in range(lax.axis_size(axis))])  56.4 us
    ppermute x13, starting transfers between devices, send(): lax.ppermute(x, axis, [(i, i ^ flip) for i in range(lax.axis_size(axis))])  53.2 us
    all_to_all x1, blocking collectives, body(): lax.all_to_all(pieces, ('box', 'src'), 0, 0, axis_index_groups=groups)  18.5 us
    dot_general x16, matrix products, forward_apply(): jnp.einsum('bsi,bij->bsj', values, block, preferred_element_type=jnp.floa...  7.4 us
    dot_general x12, matrix products, adjoint_apply(): jnp.einsum('bsj,bij->bsi', values, block, preferred_element_type=jnp.floa...  6.25 us
  transfers between devices with their start and end apart: 13, of which 8 were waited for; matrix products, arithmetic and copies ran while one was open for 14% of the time, Pallas kernels for 0%

profile of v3, /device:TPU:56, one launch (start us, length us, event | category | flops | bytes accessed | tf_op | source)
XLA Modules:
  0.0 163.1 jit_solution(3646326063724554401)
XLA Ops:
  0.8 1.8 %fusion.106 = (bf16[8,64,256]{2,1,0:T(8,128)(2,1)}, bf16[8,64,256]{2,1,0:T(8,128)(2,1)S(1)}) fusion(bf16[8,128,256]{2,1,0:T(8,128)(2,1)} %param.8), kind=kLoop, calls=%fused_computation.198 | loop fusion | bytes 1048576 | tf_op jit(solution)/shard_map/slice | solution.py:106
  3.4 10.9 %collective-permute-start = (bf16[8,72,256]{2,1,0:T(8,128)(2,1)}, bf16[8,72,256]{2,1,0:T(8,128)(2,1)S(1)}, u32[]{:S(2)}, u32[]{:S(2)}) collective-permute-start(bf16[8,72,256]{2,1,0:T(8,128)(2,1)} %pad_maximum_fusion.1), channel_id=1, source_target_pairs={{0,256},{8,264},{16,272},{24,280},{32,288},{40,296},{48,304},{56,3... | collective-permute-start | bytes 884744 | tf_op jit(solution)/shard_map/ppermute | solution.py:11
  14.3 1.9 %collective-permute-start.1 = (bf16[8,64,256]{2,1,0:T(8,128)(2,1)}, bf16[8,64,256]{2,1,0:T(8,128)(2,1)}, u32[]{:S(2)}, u32[]{:S(2)}) collective-permute-start(bf16[8,64,256]{2,1,0:T(8,128)(2,1)} %get-tuple-element.39), channel_id=1, source_target_pairs={{0,256},{8,264},{16,272},{24,280},{32,288},{40,296},{48,304},{56,3... | collective-permute-start | bytes 786440 | tf_op jit(solution)/shard_map/ppermute | solution.py:11
  16.7 4.7 %collective-permute-start.2 = (bf16[8,136,256]{2,0,1:T(8,128)(2,1)S(1)}, bf16[8,136,256]{2,0,1:T(8,128)(2,1)}, u32[]{:S(2)}, u32[]{:S(2)}) collective-permute-start(bf16[8,136,256]{2,0,1:T(8,128)(2,1)S(1)} %pad_maximum_fusion), channel_id=1, source_target_pairs={{0,64},{8,72},{16,80},{24,88},{32,96},{40,104},{48,112},{56,120},{... | collective-permute-start | bytes 1671176 | tf_op jit(solution)/shard_map/ppermute | solution.py:11
  21.4 1.8 %fusion.45 = bf16[8,128,128]{2,1,0:T(8,128)(2,1)} fusion(bf16[3,8,2,128,128]{4,3,2,1,0:T(8,128)(2,1)S(1)} %copy-done, bf16[3,8,2,128,128]{4,3,2,1,0:T(8,128)(2,1)} %param.11, pred[]{:T(512)S(6)} %ne.38, pred[]{:T(512)S(6)} %ne.37), kind=kLoop, calls=%fused_computation.106 | loop fusion | flops 393216 | bytes 1310722 | tf_op jit(solution)/shard_map/jit(_where)/select_n | solution.py:83
  23.2 5.0 %collective-permute-start.5 = (bf16[8,128,128]{2,1,0:T(8,128)(2,1)}, bf16[8,128,128]{2,1,0:T(8,128)(2,1)}, u32[]{:S(2)}, u32[]{:S(2)}) collective-permute-start(bf16[8,128,128]{2,1,0:T(8,128)(2,1)} %fusion.45), channel_id=1, source_target_pairs={{0,64},{8,72},{16,80},{24,88},{32,96},{40,104},{48,112},{56,120},{... | collective-permute-start | bytes 786440 | tf_op jit(solution)/shard_map/ppermute | solution.py:11
  28.6 1.4 copy-done.1
  31.8 1.1 fusion.22
  32.9 1.2 fusion.20
  35.1 23.6 %collective-permute-done.5 = bf16[8,128,128]{2,1,0:T(8,128)(2,1)} collective-permute-done((bf16[8,128,128]{2,1,0:T(8,128)(2,1)}, bf16[8,128,128]{2,1,0:T(8,128)(2,1)}, u32[]{:S(2)}, u32[]{:S(2)}) %collective-permute-start.5) | collective-permute-done | bytes 262176 | tf_op jit(solution)/shard_map/ppermute | solution.py:11
  58.6 3.4 %collective-permute-start.8 = (bf16[8,128,128]{2,1,0:T(8,128)(2,1)}, bf16[8,128,128]{2,1,0:T(8,128)(2,1)S(1)}, u32[]{:S(2)}, u32[]{:S(2)}) collective-permute-start(bf16[8,128,128]{2,1,0:T(8,128)(2,1)} %collective-permute-done.5), channel_id=1, source_target_pairs={{0,1},{1,0},{2,3},{3,2},{4,5},{5,4},{6,7},{7,6},{8,9},{9,8},{10,11... | collective-permute-start | bytes 786440 | tf_op jit(solution)/shard_map/ppermute | solution.py:11
  62.0 4.0 %collective-permute-start.6 = (bf16[8,128,128]{2,1,0:T(8,128)(2,1)}, bf16[8,128,128]{2,1,0:T(8,128)(2,1)S(1)}, u32[]{:S(2)}, u32[]{:S(2)}) collective-permute-start(bf16[8,128,128]{2,1,0:T(8,128)(2,1)} %collective-permute-done.5), channel_id=1, source_target_pairs={{0,3},{1,2},{2,1},{3,0},{4,7},{5,6},{6,5},{7,4},{8,11},{9,10},{10,... | collective-permute-start | bytes 786440 | tf_op jit(solution)/shard_map/ppermute | solution.py:11
  66.0 2.6 %collective-permute-start.7 = (bf16[8,128,128]{2,1,0:T(8,128)(2,1)}, bf16[8,128,128]{2,1,0:T(8,128)(2,1)S(1)}, u32[]{:S(2)}, u32[]{:S(2)}) collective-permute-start(bf16[8,128,128]{2,1,0:T(8,128)(2,1)} %collective-permute-done.5), channel_id=1, source_target_pairs={{0,2},{1,3},{2,0},{3,1},{4,6},{5,7},{6,4},{7,5},{8,10},{9,11},{10,... | collective-permute-start | bytes 786440 | tf_op jit(solution)/shard_map/ppermute | solution.py:11
  69.5 4.3 %collective-permute-start.3 = (bf16[8,64,256]{2,1,0:T(8,128)(2,1)S(1)}, bf16[8,64,256]{2,1,0:T(8,128)(2,1)S(1)}, u32[]{:S(2)}, u32[]{:S(2)}) collective-permute-start(bf16[8,64,256]{2,1,0:T(8,128)(2,1)S(1)} %fusion), channel_id=1, source_target_pairs={{0,128},{8,136},{16,144},{24,152},{32,160},{40,168},{48,176},{56,1... | collective-permute-start | bytes 786440 | tf_op jit(solution)/shard_map/ppermute | solution.py:11
  73.8 1.3 fusion.5
  75.4 2.5 %collective-permute-start.10 = (bf16[8,64,256]{2,1,0:T(8,128)(2,1)S(1)}, bf16[8,64,256]{2,1,0:T(8,128)(2,1)S(1)}, u32[]{:S(2)}, u32[]{:S(2)}) collective-permute-start(bf16[8,64,256]{2,1,0:T(8,128)(2,1)S(1)} %fusion.5), channel_id=1, source_target_pairs={{0,128},{8,136},{16,144},{24,152},{32,160},{40,168},{48,176},{56,1... | collective-permute-start | bytes 786440 | tf_op jit(solution)/shard_map/ppermute | solution.py:11
  78.6 1.1 fusion.101
  79.7 12.2 %collective-permute-done.3 = bf16[8,64,256]{2,1,0:T(8,128)(2,1)S(1)} collective-permute-done((bf16[8,64,256]{2,1,0:T(8,128)(2,1)S(1)}, bf16[8,64,256]{2,1,0:T(8,128)(2,1)S(1)}, u32[]{:S(2)}, u32[]{:S(2)}) %collective-permute-start.3) | collective-permute-done | bytes 262176 | tf_op jit(solution)/shard_map/ppermute | solution.py:11
  92.3 1.9 %collective-permute-start.4 = (bf16[8,64,256]{2,1,0:T(8,128)(2,1)S(1)}, bf16[8,64,256]{2,1,0:T(8,128)(2,1)S(1)}, u32[]{:S(2)}, u32[]{:S(2)}) collective-permute-start(bf16[8,64,256]{2,1,0:T(8,128)(2,1)S(1)} %fusion.1), channel_id=1, source_target_pairs={{0,64},{8,72},{16,80},{24,88},{32,96},{40,104},{48,112},{56,120},{... | collective-permute-start | bytes 786440 | tf_op jit(solution)/shard_map/ppermute | solution.py:11
  94.5 2.0 %collective-permute-done.10 = bf16[8,64,256]{2,1,0:T(8,128)(2,1)S(1)} collective-permute-done((bf16[8,64,256]{2,1,0:T(8,128)(2,1)S(1)}, bf16[8,64,256]{2,1,0:T(8,128)(2,1)S(1)}, u32[]{:S(2)}, u32[]{:S(2)}) %collective-permute-start.10) | collective-permute-done | bytes 262176 | tf_op jit(solution)/shard_map/ppermute | solution.py:11
  97.1 5.9 %collective-permute-start.11 = (bf16[8,64,256]{2,1,0:T(8,128)(2,1)S(1)}, bf16[8,64,256]{2,1,0:T(8,128)(2,1)S(1)}, u32[]{:S(2)}, u32[]{:S(2)}) collective-permute-start(bf16[8,64,256]{2,1,0:T(8,128)(2,1)S(1)} %fusion.6), channel_id=1, source_target_pairs={{0,64},{8,72},{16,80},{24,88},{32,96},{40,104},{48,112},{56,120},{... | collective-permute-start | bytes 786440 | tf_op jit(solution)/shard_map/ppermute | solution.py:11
  103.3 1.1 fusion.105
  104.8 6.9 %collective-permute-done.4 = bf16[8,64,256]{2,1,0:T(8,128)(2,1)S(1)} collective-permute-done((bf16[8,64,256]{2,1,0:T(8,128)(2,1)S(1)}, bf16[8,64,256]{2,1,0:T(8,128)(2,1)S(1)}, u32[]{:S(2)}, u32[]{:S(2)}) %collective-permute-start.4) | collective-permute-done | bytes 262176 | tf_op jit(solution)/shard_map/ppermute | solution.py:11
  112.6 0.9 convolution_subtract_fusion.1
  114.3 0.9 convolution_convert_fusion.4
  116.2 1.9 %collective-permute-start.9 = (bf16[8,64,256]{2,1,0:T(8,128)(2,1)S(1)}, bf16[8,64,256]{2,1,0:T(8,128)(2,1)S(1)}, u32[]{:S(2)}, u32[]{:S(2)}) collective-permute-start(bf16[8,64,256]{2,1,0:T(8,128)(2,1)S(1)} %convolution_convert_fusion.3), channel_id=1, source_target_pairs={{0,128},{8,136},{16,144},{24,152},{32,160},{40,168},{48,176},{56,1... | collective-permute-start | bytes 786440 | tf_op jit(solution)/shard_map/ppermute | solution.py:11
  122.0 0.9 convolution_convert_fusion.1
  123.8 4.2 %collective-permute-start.12 = (bf16[8,64,256]{2,1,0:T(8,128)(2,1)S(1)}, bf16[8,64,256]{2,1,0:T(8,128)(2,1)S(1)}, u32[]{:S(2)}, u32[]{:S(2)}) collective-permute-start(bf16[8,64,256]{2,1,0:T(8,128)(2,1)S(1)} %convolution_convert_fusion), channel_id=1, source_target_pairs={{0,128},{8,136},{16,144},{24,152},{32,160},{40,168},{48,176},{56,1... | collective-permute-start | bytes 786440 | tf_op jit(solution)/shard_map/ppermute | solution.py:11
  128.5 4.2 %collective-permute-done.9 = bf16[8,64,256]{2,1,0:T(8,128)(2,1)S(1)} collective-permute-done((bf16[8,64,256]{2,1,0:T(8,128)(2,1)S(1)}, bf16[8,64,256]{2,1,0:T(8,128)(2,1)S(1)}, u32[]{:S(2)}, u32[]{:S(2)}) %collective-permute-start.9) | collective-permute-done | bytes 262176 | tf_op jit(solution)/shard_map/ppermute | solution.py:11
  133.2 6.1 %collective-permute-done.12 = bf16[8,64,256]{2,1,0:T(8,128)(2,1)S(1)} collective-permute-done((bf16[8,64,256]{2,1,0:T(8,128)(2,1)S(1)}, bf16[8,64,256]{2,1,0:T(8,128)(2,1)S(1)}, u32[]{:S(2)}, u32[]{:S(2)}) %collective-permute-start.12) | collective-permute-done | bytes 262176 | tf_op jit(solution)/shard_map/ppermute | solution.py:11
  141.0 1.4 convert_multiply_fusion.2
  142.7 18.5 %all_to_all.5 = f32[16,1,128]{2,1,0:T(1,128)S(1)} all-to-all(f32[16,1,128]{2,1,0:T(1,128)S(1)} %reshape.97), channel_id=1, replica_groups={{0,1,2,3,4,5,6,7,256,257,258,259,260,261,262,263},{8,9,10,11,12,13,14,1..., dimensions={0} | all-to-all | bytes 16384 | tf_op jit(solution)/shard_map/all_to_all | solution.py:170
  (145 shorter events, 20.7 us)
Async XLA Ops:
  0.0 16.2 %copy-start.2 = (bf16[8,128,256]{2,1,0:T(8,128)(2,1)S(1)}, bf16[8,128,256]{2,1,0:T(8,128)(2,1)}, u32[]{:S(2)}) copy-start(bf16[8,128,256]{2,1,0:T(8,128)(2,1)} %param.13) | copy-start | bytes 1572868
  0.0 16.5 %copy-start.19 = (s32[8]{0:T(128)S(1)}, s32[8]{0:T(128)}, u32[]{:S(2)}) copy-start(s32[8]{0:T(128)} %param.12) | copy-start | bytes 100
  2.6 18.8 %copy-start = (bf16[3,8,2,128,128]{4,3,2,1,0:T(8,128)(2,1)S(1)}, bf16[3,8,2,128,128]{4,3,2,1,0:T(8,128)(2,1)}, u32[]{:S(2)}) copy-start(bf16[3,8,2,128,128]{4,3,2,1,0:T(8,128)(2,1)} %param.10) | copy-start | bytes 4718596
  3.4 62.7 %collective-permute-start = (bf16[8,72,256]{2,1,0:T(8,128)(2,1)}, bf16[8,72,256]{2,1,0:T(8,128)(2,1)S(1)}, u32[]{:S(2)}, u32[]{:S(2)}) collective-permute-start(bf16[8,72,256]{2,1,0:T(8,128)(2,1)} %pad_maximum_fusion.1), channel_id=1, source_target_pairs={{0,256},{8,264},{16,272},{24,280},{32,288},{40,296},{48,304},{56,3... | collective-permute-start | bytes 884744 | tf_op jit(solution)/shard_map/ppermute | solution.py:11
  14.3 55.2 %collective-permute-start.1 = (bf16[8,64,256]{2,1,0:T(8,128)(2,1)}, bf16[8,64,256]{2,1,0:T(8,128)(2,1)}, u32[]{:S(2)}, u32[]{:S(2)}) collective-permute-start(bf16[8,64,256]{2,1,0:T(8,128)(2,1)} %get-tuple-element.39), channel_id=1, source_target_pairs={{0,256},{8,264},{16,272},{24,280},{32,288},{40,296},{48,304},{56,3... | collective-permute-start | bytes 786440 | tf_op jit(solution)/shard_map/ppermute | solution.py:11
  16.2 12.1 %copy-start.18 = (f32[8,128]{1,0:T(8,128)S(1)}, f32[8,128]{1,0:T(8,128)}, u32[]{:S(2)}) copy-start(f32[8,128]{1,0:T(8,128)} %param.9) | copy-start | bytes 12292
  16.7 86.7 %collective-permute-start.2 = (bf16[8,136,256]{2,0,1:T(8,128)(2,1)S(1)}, bf16[8,136,256]{2,0,1:T(8,128)(2,1)}, u32[]{:S(2)}, u32[]{:S(2)}) collective-permute-start(bf16[8,136,256]{2,0,1:T(8,128)(2,1)S(1)} %pad_maximum_fusion), channel_id=1, source_target_pairs={{0,64},{8,72},{16,80},{24,88},{32,96},{40,104},{48,112},{56,120},{... | collective-permute-start | bytes 1671176 | tf_op jit(solution)/shard_map/ppermute | solution.py:11
  23.2 35.4 %collective-permute-start.5 = (bf16[8,128,128]{2,1,0:T(8,128)(2,1)}, bf16[8,128,128]{2,1,0:T(8,128)(2,1)}, u32[]{:S(2)}, u32[]{:S(2)}) collective-permute-start(bf16[8,128,128]{2,1,0:T(8,128)(2,1)} %fusion.45), channel_id=1, source_target_pairs={{0,64},{8,72},{16,80},{24,88},{32,96},{40,104},{48,112},{56,120},{... | collective-permute-start | bytes 786440 | tf_op jit(solution)/shard_map/ppermute | solution.py:11
  34.9 33.7 %copy-start.6 = (bf16[8,128,128]{2,1,0:T(8,128)(2,1)S(1)}, bf16[8,128,128]{2,1,0:T(8,128)(2,1)}, u32[]{:S(2)}) copy-start(bf16[8,128,128]{2,1,0:T(8,128)(2,1)} %fusion.87) | copy-start | bytes 786436
  34.9 33.7 %copy-start.10 = (bf16[8,128,128]{2,1,0:T(8,128)(2,1)S(1)}, bf16[8,128,128]{2,1,0:T(8,128)(2,1)}, u32[]{:S(2)}) copy-start(bf16[8,128,128]{2,1,0:T(8,128)(2,1)} %get-tuple-element.49) | copy-start | bytes 786436
  34.9 33.7 %copy-start.12 = (bf16[8,128,128]{2,1,0:T(8,128)(2,1)S(1)}, bf16[8,128,128]{2,1,0:T(8,128)(2,1)}, u32[]{:S(2)}) copy-start(bf16[8,128,128]{2,1,0:T(8,128)(2,1)} %get-tuple-element.50) | copy-start | bytes 786436
  34.9 33.7 %copy-start.27 = (f32[8,64,256]{2,1,0:T(8,128)S(1)}, f32[8,64,256]{2,1,0:T(8,128)}, u32[]{:S(2)}) copy-start(f32[8,64,256]{2,1,0:T(8,128)} %fusion.22) | copy-start | bytes 1572868
  58.6 16.8 %collective-permute-start.8 = (bf16[8,128,128]{2,1,0:T(8,128)(2,1)}, bf16[8,128,128]{2,1,0:T(8,128)(2,1)S(1)}, u32[]{:S(2)}, u32[]{:S(2)}) collective-permute-start(bf16[8,128,128]{2,1,0:T(8,128)(2,1)} %collective-permute-done.5), channel_id=1, source_target_pairs={{0,1},{1,0},{2,3},{3,2},{4,5},{5,4},{6,7},{7,6},{8,9},{9,8},{10,11... | collective-permute-start | bytes 786440 | tf_op jit(solution)/shard_map/ppermute | solution.py:11
  62.0 16.6 %collective-permute-start.6 = (bf16[8,128,128]{2,1,0:T(8,128)(2,1)}, bf16[8,128,128]{2,1,0:T(8,128)(2,1)S(1)}, u32[]{:S(2)}, u32[]{:S(2)}) collective-permute-start(bf16[8,128,128]{2,1,0:T(8,128)(2,1)} %collective-permute-done.5), channel_id=1, source_target_pairs={{0,3},{1,2},{2,1},{3,0},{4,7},{5,6},{6,5},{7,4},{8,11},{9,10},{10,... | collective-permute-start | bytes 786440 | tf_op jit(solution)/shard_map/ppermute | solution.py:11
  66.0 9.0 %copy-start.5 = (bf16[8,72,256]{2,1,0:T(8,128)(2,1)}, bf16[8,72,256]{2,1,0:T(8,128)(2,1)S(1)}, u32[]{:S(2)}) copy-start(bf16[8,72,256]{2,1,0:T(8,128)(2,1)S(1)} %collective-permute-done) | copy-start | bytes 884740
  66.0 12.6 %collective-permute-start.7 = (bf16[8,128,128]{2,1,0:T(8,128)(2,1)}, bf16[8,128,128]{2,1,0:T(8,128)(2,1)S(1)}, u32[]{:S(2)}, u32[]{:S(2)}) collective-permute-start(bf16[8,128,128]{2,1,0:T(8,128)(2,1)} %collective-permute-done.5), channel_id=1, source_target_pairs={{0,2},{1,3},{2,0},{3,1},{4,6},{5,7},{6,4},{7,5},{8,10},{9,11},{10,... | collective-permute-start | bytes 786440 | tf_op jit(solution)/shard_map/ppermute | solution.py:11
  69.5 22.4 %collective-permute-start.3 = (bf16[8,64,256]{2,1,0:T(8,128)(2,1)S(1)}, bf16[8,64,256]{2,1,0:T(8,128)(2,1)S(1)}, u32[]{:S(2)}, u32[]{:S(2)}) collective-permute-start(bf16[8,64,256]{2,1,0:T(8,128)(2,1)S(1)} %fusion), channel_id=1, source_target_pairs={{0,128},{8,136},{16,144},{24,152},{32,160},{40,168},{48,176},{56,1... | collective-permute-start | bytes 786440 | tf_op jit(solution)/shard_map/ppermute | solution.py:11
  75.4 21.1 %collective-permute-start.10 = (bf16[8,64,256]{2,1,0:T(8,128)(2,1)S(1)}, bf16[8,64,256]{2,1,0:T(8,128)(2,1)S(1)}, u32[]{:S(2)}, u32[]{:S(2)}) collective-permute-start(bf16[8,64,256]{2,1,0:T(8,128)(2,1)S(1)} %fusion.5), channel_id=1, source_target_pairs={{0,128},{8,136},{16,144},{24,152},{32,160},{40,168},{48,176},{56,1... | collective-permute-start | bytes 786440 | tf_op jit(solution)/shard_map/ppermute | solution.py:11
  92.3 19.4 %collective-permute-start.4 = (bf16[8,64,256]{2,1,0:T(8,128)(2,1)S(1)}, bf16[8,64,256]{2,1,0:T(8,128)(2,1)S(1)}, u32[]{:S(2)}, u32[]{:S(2)}) collective-permute-start(bf16[8,64,256]{2,1,0:T(8,128)(2,1)S(1)} %fusion.1), channel_id=1, source_target_pairs={{0,64},{8,72},{16,80},{24,88},{32,96},{40,104},{48,112},{56,120},{... | collective-permute-start | bytes 786440 | tf_op jit(solution)/shard_map/ppermute | solution.py:11
  97.1 22.2 %collective-permute-start.11 = (bf16[8,64,256]{2,1,0:T(8,128)(2,1)S(1)}, bf16[8,64,256]{2,1,0:T(8,128)(2,1)S(1)}, u32[]{:S(2)}, u32[]{:S(2)}) collective-permute-start(bf16[8,64,256]{2,1,0:T(8,128)(2,1)S(1)} %fusion.6), channel_id=1, source_target_pairs={{0,64},{8,72},{16,80},{24,88},{32,96},{40,104},{48,112},{56,120},{... | collective-permute-start | bytes 786440 | tf_op jit(solution)/shard_map/ppermute | solution.py:11
  116.2 16.5 %collective-permute-start.9 = (bf16[8,64,256]{2,1,0:T(8,128)(2,1)S(1)}, bf16[8,64,256]{2,1,0:T(8,128)(2,1)S(1)}, u32[]{:S(2)}, u32[]{:S(2)}) collective-permute-start(bf16[8,64,256]{2,1,0:T(8,128)(2,1)S(1)} %convolution_convert_fusion.3), channel_id=1, source_target_pairs={{0,128},{8,136},{16,144},{24,152},{32,160},{40,168},{48,176},{56,1... | collective-permute-start | bytes 786440 | tf_op jit(solution)/shard_map/ppermute | solution.py:11
  118.5 14.2 %copy-start.22 = (f32[8,64,256]{2,1,0:T(8,128)}, f32[8,64,256]{2,1,0:T(8,128)S(1)}, u32[]{:S(2)}) copy-start(f32[8,64,256]{2,1,0:T(8,128)S(1)} %fusion.99) | copy-start | bytes 1572868
  123.8 8.9 %copy-start.4 = (bf16[8,128,256]{2,1,0:T(8,128)(2,1)S(1)}, bf16[8,128,256]{2,1,0:T(8,128)(2,1)}, u32[]{:S(2)}) copy-start(bf16[8,128,256]{2,1,0:T(8,128)(2,1)} %param.8) | copy-start | bytes 1572868
  123.8 8.9 %copy-start.9 = (bf16[8,128,128]{2,1,0:T(8,128)(2,1)S(1)}, bf16[8,128,128]{2,1,0:T(8,128)(2,1)}, u32[]{:S(2)}) copy-start(bf16[8,128,128]{2,1,0:T(8,128)(2,1)} %copy-done.8) | copy-start | bytes 786436
  123.8 8.9 %copy-start.15 = (bf16[8,128,128]{2,1,0:T(8,128)(2,1)S(1)}, bf16[8,128,128]{2,1,0:T(8,128)(2,1)}, u32[]{:S(2)}) copy-start(bf16[8,128,128]{2,1,0:T(8,128)(2,1)} %copy-done.14) | copy-start | bytes 786436
  123.8 8.9 %copy-start.17 = (bf16[8,128,128]{2,1,0:T(8,128)(2,1)S(1)}, bf16[8,128,128]{2,1,0:T(8,128)(2,1)}, u32[]{:S(2)}) copy-start(bf16[8,128,128]{2,1,0:T(8,128)(2,1)} %copy-done.16) | copy-start | bytes 786436
  123.8 15.5 %collective-permute-start.12 = (bf16[8,64,256]{2,1,0:T(8,128)(2,1)S(1)}, bf16[8,64,256]{2,1,0:T(8,128)(2,1)S(1)}, u32[]{:S(2)}, u32[]{:S(2)}) collective-permute-start(bf16[8,64,256]{2,1,0:T(8,128)(2,1)S(1)} %convolution_convert_fusion), channel_id=1, source_target_pairs={{0,128},{8,136},{16,144},{24,152},{32,160},{40,168},{48,176},{56,1... | collective-permute-start | bytes 786440 | tf_op jit(solution)/shard_map/ppermute | solution.py:11
  128.5 10.9 %copy-start.24 = (f32[8,64,256]{2,1,0:T(8,128)}, f32[8,64,256]{2,1,0:T(8,128)S(1)}, u32[]{:S(2)}) copy-start(f32[8,64,256]{2,1,0:T(8,128)S(1)} %fusion.97) | copy-start | bytes 1572868
  133.2 6.8 %slice-start = ((bf16[8,72,256]{2,1,0:T(8,128)(2,1)}), bf16[8,64,256]{2,1,0:T(8,128)(2,1)S(1)}, s32[]{:S(2)}) async-start(bf16[8,72,256]{2,1,0:T(8,128)(2,1)} %copy-done.5), calls=%async_computation.1 | async-start | bytes 524288 | tf_op jit(solution)/shard_map/slice | solution.py:111
  133.2 6.7 %copy-start.7 = (bf16[8,128,128]{2,1,0:T(8,128)(2,1)S(1)}, bf16[8,128,128]{2,1,0:T(8,128)(2,1)}, u32[]{:S(2)}) copy-start(bf16[8,128,128]{2,1,0:T(8,128)(2,1)} %fusion.87) | copy-start | bytes 786436
  133.2 6.7 %copy-start.11 = (bf16[8,128,128]{2,1,0:T(8,128)(2,1)S(1)}, bf16[8,128,128]{2,1,0:T(8,128)(2,1)}, u32[]{:S(2)}) copy-start(bf16[8,128,128]{2,1,0:T(8,128)(2,1)} %get-tuple-element.49) | copy-start | bytes 786436
  133.2 6.7 %copy-start.13 = (bf16[8,128,128]{2,1,0:T(8,128)(2,1)S(1)}, bf16[8,128,128]{2,1,0:T(8,128)(2,1)}, u32[]{:S(2)}) copy-start(bf16[8,128,128]{2,1,0:T(8,128)(2,1)} %get-tuple-element.50) | copy-start | bytes 786436
  (10 other events, 28.7 us)

commit v4 on v3

--- a/solution.py
+++ b/solution.py
@@ -103,9 +103,12 @@
     assert ends[-1] == source_count
     spans = [slice(end - size, end) for end, size in zip(ends, CHUNKS)]
 
-    incidents = [incident[:, span] for span in spans]
-    sent = list(incidents)
-    sent[0] = jnp.concatenate([sent[0], split_gains(reflectivity)], axis=1)
+    incidents = [incident[:, spans[0]]]
+    sent = [jnp.concatenate([incidents[0], split_gains(reflectivity)], axis=1)]
+    for span in spans[1:]:
+        later, _ = lax.optimization_barrier((incident, sent[-1]))
+        incidents.append(later[:, span])
+        sent.append(incidents[-1])
     came = [send(x, "box", flip0) for x in sent]
     across_gains = join_gains(came[0][:, CHUNKS[0] :])
     across_incidents = [x[:, :size] for x, size in zip(came, CHUNKS)]

time: 164 us -> 165 us (level)
  transfers between devices with their start and end apart: 13 -> 13, of which waited for: 8 -> 8; matrix products, arithmetic and copies ran while one was open for 14% -> 15% of each run, Pallas kernels for 0% -> 0%
where the time goes in v4:
time: 165 us; the launch traced here: 164 us
  waiting for transfers between devices  56.5 us (34%)
  starting transfers between devices  53.2 us (32%)
  blocking collectives  18.6 us (11%)
  matrix products  18.4 us (11%)
  local copies, waits for them, and re-layouts  9.1 us (6%)
  other arithmetic  7.48 us (5%)
    ppermute x13, waiting for transfers between devices, send(): lax.ppermute(x, axis, [(i, i ^ flip) for i in range(lax.axis_size(axis))])  56.5 us
    ppermute x13, starting transfers between devices, send(): lax.ppermute(x, axis, [(i, i ^ flip) for i in range(lax.axis_size(axis))])  53.2 us
    all_to_all x1, blocking collectives, body(): lax.all_to_all(pieces, ('box', 'src'), 0, 0, axis_index_groups=groups)  18.6 us
    dot_general x16, matrix products, forward_apply(): jnp.einsum('bsi,bij->bsj', values, block, preferred_element_type=jnp.floa...  7.38 us
    dot_general x12, matrix products, adjoint_apply(): jnp.einsum('bsj,bij->bsi', values, block, preferred_element_type=jnp.floa...  6.25 us
  transfers between devices with their start and end apart: 13, of which 8 were waited for; matrix products, arithmetic and copies ran while one was open for 15% of the time, Pallas kernels for 0%

profile of v4, /device:TPU:56, one launch (start us, length us, event | category | flops | bytes accessed | tf_op | source)
XLA Modules:
  0.0 164.0 jit_solution(3098196892901339347)
XLA Ops:
  0.8 1.0 slice.161
  2.5 10.9 %collective-permute-start = (bf16[8,72,256]{2,1,0:T(8,128)(2,1)}, bf16[8,72,256]{2,1,0:T(8,128)(2,1)S(1)}, u32[]{:S(2)}, u32[]{:S(2)}) collective-permute-start(bf16[8,72,256]{2,1,0:T(8,128)(2,1)} %pad_maximum_fusion.1), channel_id=1, source_target_pairs={{0,256},{8,264},{16,272},{24,280},{32,288},{40,296},{48,304},{56,3... | collective-permute-start | bytes 884744 | tf_op jit(solution)/shard_map/ppermute | solution.py:11
  13.5 1.7 %slice.163 = bf16[8,64,256]{2,1,0:T(8,128)(2,1)} slice(bf16[8,128,256]{2,1,0:T(8,128)(2,1)} %param.8), slice={[0:8], [64:128], [0:256]} | slice | bytes 524288 | tf_op jit(solution)/shard_map/slice | solution.py:110
  15.1 1.9 %collective-permute-start.1 = (bf16[8,64,256]{2,1,0:T(8,128)(2,1)}, bf16[8,64,256]{2,1,0:T(8,128)(2,1)}, u32[]{:S(2)}, u32[]{:S(2)}) collective-permute-start(bf16[8,64,256]{2,1,0:T(8,128)(2,1)} %slice.163), channel_id=1, source_target_pairs={{0,256},{8,264},{16,272},{24,280},{32,288},{40,296},{48,304},{56,3... | collective-permute-start | bytes 786440 | tf_op jit(solution)/shard_map/ppermute | solution.py:11
  17.5 4.7 %collective-permute-start.2 = (bf16[8,136,256]{2,0,1:T(8,128)(2,1)S(1)}, bf16[8,136,256]{2,0,1:T(8,128)(2,1)}, u32[]{:S(2)}, u32[]{:S(2)}) collective-permute-start(bf16[8,136,256]{2,0,1:T(8,128)(2,1)S(1)} %pad_maximum_fusion), channel_id=1, source_target_pairs={{0,64},{8,72},{16,80},{24,88},{32,96},{40,104},{48,112},{56,120},{... | collective-permute-start | bytes 1671176 | tf_op jit(solution)/shard_map/ppermute | solution.py:11
  22.3 1.8 %fusion.45 = bf16[8,128,128]{2,1,0:T(8,128)(2,1)} fusion(bf16[3,8,2,128,128]{4,3,2,1,0:T(8,128)(2,1)S(1)} %copy-done, bf16[3,8,2,128,128]{4,3,2,1,0:T(8,128)(2,1)} %param.11, pred[]{:T(512)S(6)} %ne.38, pred[]{:T(512)S(6)} %ne.37), kind=kLoop, calls=%fused_computation.106 | loop fusion | flops 393216 | bytes 1310722 | tf_op jit(solution)/shard_map/jit(_where)/select_n | solution.py:83
  24.1 5.0 %collective-permute-start.5 = (bf16[8,128,128]{2,1,0:T(8,128)(2,1)}, bf16[8,128,128]{2,1,0:T(8,128)(2,1)}, u32[]{:S(2)}, u32[]{:S(2)}) collective-permute-start(bf16[8,128,128]{2,1,0:T(8,128)(2,1)} %fusion.45), channel_id=1, source_target_pairs={{0,64},{8,72},{16,80},{24,88},{32,96},{40,104},{48,112},{56,120},{... | collective-permute-start | bytes 786440 | tf_op jit(solution)/shard_map/ppermute | solution.py:11
  29.4 1.4 copy-done.1
  32.6 1.1 fusion.22
  33.8 1.1 fusion.20
  35.9 23.6 %collective-permute-done.5 = bf16[8,128,128]{2,1,0:T(8,128)(2,1)} collective-permute-done((bf16[8,128,128]{2,1,0:T(8,128)(2,1)}, bf16[8,128,128]{2,1,0:T(8,128)(2,1)}, u32[]{:S(2)}, u32[]{:S(2)}) %collective-permute-start.5) | collective-permute-done | bytes 262176 | tf_op jit(solution)/shard_map/ppermute | solution.py:11
  59.5 3.4 %collective-permute-start.8 = (bf16[8,128,128]{2,1,0:T(8,128)(2,1)}, bf16[8,128,128]{2,1,0:T(8,128)(2,1)S(1)}, u32[]{:S(2)}, u32[]{:S(2)}) collective-permute-start(bf16[8,128,128]{2,1,0:T(8,128)(2,1)} %collective-permute-done.5), channel_id=1, source_target_pairs={{0,1},{1,0},{2,3},{3,2},{4,5},{5,4},{6,7},{7,6},{8,9},{9,8},{10,11... | collective-permute-start | bytes 786440 | tf_op jit(solution)/shard_map/ppermute | solution.py:11
  62.8 4.0 %collective-permute-start.6 = (bf16[8,128,128]{2,1,0:T(8,128)(2,1)}, bf16[8,128,128]{2,1,0:T(8,128)(2,1)S(1)}, u32[]{:S(2)}, u32[]{:S(2)}) collective-permute-start(bf16[8,128,128]{2,1,0:T(8,128)(2,1)} %collective-permute-done.5), channel_id=1, source_target_pairs={{0,3},{1,2},{2,1},{3,0},{4,7},{5,6},{6,5},{7,4},{8,11},{9,10},{10,... | collective-permute-start | bytes 786440 | tf_op jit(solution)/shard_map/ppermute | solution.py:11
  66.9 2.6 %collective-permute-start.7 = (bf16[8,128,128]{2,1,0:T(8,128)(2,1)}, bf16[8,128,128]{2,1,0:T(8,128)(2,1)S(1)}, u32[]{:S(2)}, u32[]{:S(2)}) collective-permute-start(bf16[8,128,128]{2,1,0:T(8,128)(2,1)} %collective-permute-done.5), channel_id=1, source_target_pairs={{0,2},{1,3},{2,0},{3,1},{4,6},{5,7},{6,4},{7,5},{8,10},{9,11},{10,... | collective-permute-start | bytes 786440 | tf_op jit(solution)/shard_map/ppermute | solution.py:11
  70.3 4.3 %collective-permute-start.3 = (bf16[8,64,256]{2,1,0:T(8,128)(2,1)S(1)}, bf16[8,64,256]{2,1,0:T(8,128)(2,1)S(1)}, u32[]{:S(2)}, u32[]{:S(2)}) collective-permute-start(bf16[8,64,256]{2,1,0:T(8,128)(2,1)S(1)} %fusion), channel_id=1, source_target_pairs={{0,128},{8,136},{16,144},{24,152},{32,160},{40,168},{48,176},{56,1... | collective-permute-start | bytes 786440 | tf_op jit(solution)/shard_map/ppermute | solution.py:11
  74.6 1.3 fusion.5
  76.2 2.5 %collective-permute-start.10 = (bf16[8,64,256]{2,1,0:T(8,128)(2,1)S(1)}, bf16[8,64,256]{2,1,0:T(8,128)(2,1)S(1)}, u32[]{:S(2)}, u32[]{:S(2)}) collective-permute-start(bf16[8,64,256]{2,1,0:T(8,128)(2,1)S(1)} %fusion.5), channel_id=1, source_target_pairs={{0,128},{8,136},{16,144},{24,152},{32,160},{40,168},{48,176},{56,1... | collective-permute-start | bytes 786440 | tf_op jit(solution)/shard_map/ppermute | solution.py:11
  79.5 1.1 fusion.101
  80.6 12.2 %collective-permute-done.3 = bf16[8,64,256]{2,1,0:T(8,128)(2,1)S(1)} collective-permute-done((bf16[8,64,256]{2,1,0:T(8,128)(2,1)S(1)}, bf16[8,64,256]{2,1,0:T(8,128)(2,1)S(1)}, u32[]{:S(2)}, u32[]{:S(2)}) %collective-permute-start.3) | collective-permute-done | bytes 262176 | tf_op jit(solution)/shard_map/ppermute | solution.py:11
  93.1 1.9 %collective-permute-start.4 = (bf16[8,64,256]{2,1,0:T(8,128)(2,1)S(1)}, bf16[8,64,256]{2,1,0:T(8,128)(2,1)S(1)}, u32[]{:S(2)}, u32[]{:S(2)}) collective-permute-start(bf16[8,64,256]{2,1,0:T(8,128)(2,1)S(1)} %fusion.1), channel_id=1, source_target_pairs={{0,64},{8,72},{16,80},{24,88},{32,96},{40,104},{48,112},{56,120},{... | collective-permute-start | bytes 786440 | tf_op jit(solution)/shard_map/ppermute | solution.py:11
  95.4 2.0 %collective-permute-done.10 = bf16[8,64,256]{2,1,0:T(8,128)(2,1)S(1)} collective-permute-done((bf16[8,64,256]{2,1,0:T(8,128)(2,1)S(1)}, bf16[8,64,256]{2,1,0:T(8,128)(2,1)S(1)}, u32[]{:S(2)}, u32[]{:S(2)}) %collective-permute-start.10) | collective-permute-done | bytes 262176 | tf_op jit(solution)/shard_map/ppermute | solution.py:11
  98.0 5.9 %collective-permute-start.11 = (bf16[8,64,256]{2,1,0:T(8,128)(2,1)S(1)}, bf16[8,64,256]{2,1,0:T(8,128)(2,1)S(1)}, u32[]{:S(2)}, u32[]{:S(2)}) collective-permute-start(bf16[8,64,256]{2,1,0:T(8,128)(2,1)S(1)} %fusion.6), channel_id=1, source_target_pairs={{0,64},{8,72},{16,80},{24,88},{32,96},{40,104},{48,112},{56,120},{... | collective-permute-start | bytes 786440 | tf_op jit(solution)/shard_map/ppermute | solution.py:11
  104.2 1.1 fusion.105
  105.6 6.9 %collective-permute-done.4 = bf16[8,64,256]{2,1,0:T(8,128)(2,1)S(1)} collective-permute-done((bf16[8,64,256]{2,1,0:T(8,128)(2,1)S(1)}, bf16[8,64,256]{2,1,0:T(8,128)(2,1)S(1)}, u32[]{:S(2)}, u32[]{:S(2)}) %collective-permute-start.4) | collective-permute-done | bytes 262176 | tf_op jit(solution)/shard_map/ppermute | solution.py:11
  115.2 0.9 convolution_convert_fusion.4
  117.0 1.9 %collective-permute-start.9 = (bf16[8,64,256]{2,1,0:T(8,128)(2,1)S(1)}, bf16[8,64,256]{2,1,0:T(8,128)(2,1)S(1)}, u32[]{:S(2)}, u32[]{:S(2)}) collective-permute-start(bf16[8,64,256]{2,1,0:T(8,128)(2,1)S(1)} %convolution_convert_fusion.3), channel_id=1, source_target_pairs={{0,128},{8,136},{16,144},{24,152},{32,160},{40,168},{48,176},{56,1... | collective-permute-start | bytes 786440 | tf_op jit(solution)/shard_map/ppermute | solution.py:11
  122.8 0.9 convolution_convert_fusion.1
  124.7 4.2 %collective-permute-start.12 = (bf16[8,64,256]{2,1,0:T(8,128)(2,1)S(1)}, bf16[8,64,256]{2,1,0:T(8,128)(2,1)S(1)}, u32[]{:S(2)}, u32[]{:S(2)}) collective-permute-start(bf16[8,64,256]{2,1,0:T(8,128)(2,1)S(1)} %convolution_convert_fusion), channel_id=1, source_target_pairs={{0,128},{8,136},{16,144},{24,152},{32,160},{40,168},{48,176},{56,1... | collective-permute-start | bytes 786440 | tf_op jit(solution)/shard_map/ppermute | solution.py:11
  129.3 4.1 %collective-permute-done.9 = bf16[8,64,256]{2,1,0:T(8,128)(2,1)S(1)} collective-permute-done((bf16[8,64,256]{2,1,0:T(8,128)(2,1)S(1)}, bf16[8,64,256]{2,1,0:T(8,128)(2,1)S(1)}, u32[]{:S(2)}, u32[]{:S(2)}) %collective-permute-start.9) | collective-permute-done | bytes 262176 | tf_op jit(solution)/shard_map/ppermute | solution.py:11
  134.0 6.2 %collective-permute-done.12 = bf16[8,64,256]{2,1,0:T(8,128)(2,1)S(1)} collective-permute-done((bf16[8,64,256]{2,1,0:T(8,128)(2,1)S(1)}, bf16[8,64,256]{2,1,0:T(8,128)(2,1)S(1)}, u32[]{:S(2)}, u32[]{:S(2)}) %collective-permute-start.12) | collective-permute-done | bytes 262176 | tf_op jit(solution)/shard_map/ppermute | solution.py:11
  141.9 1.4 convert_multiply_fusion.2
  143.5 18.6 %all_to_all.5 = f32[16,1,128]{2,1,0:T(1,128)S(1)} all-to-all(f32[16,1,128]{2,1,0:T(1,128)S(1)} %reshape.97), channel_id=1, replica_groups={{0,1,2,3,4,5,6,7,256,257,258,259,260,261,262,263},{8,9,10,11,12,13,14,1..., dimensions={0} | all-to-all | bytes 16384 | tf_op jit(solution)/shard_map/all_to_all | solution.py:173
  (146 shorter events, 21.7 us)
Async XLA Ops:
  0.0 17.0 %copy-start.2 = (bf16[8,128,256]{2,1,0:T(8,128)(2,1)S(1)}, bf16[8,128,256]{2,1,0:T(8,128)(2,1)}, u32[]{:S(2)}) copy-start(bf16[8,128,256]{2,1,0:T(8,128)(2,1)} %param.13) | copy-start | bytes 1572868
  0.0 17.4 %copy-start.19 = (s32[8]{0:T(128)S(1)}, s32[8]{0:T(128)}, u32[]{:S(2)}) copy-start(s32[8]{0:T(128)} %param.12) | copy-start | bytes 100
  1.8 20.5 %copy-start = (bf16[3,8,2,128,128]{4,3,2,1,0:T(8,128)(2,1)S(1)}, bf16[3,8,2,128,128]{4,3,2,1,0:T(8,128)(2,1)}, u32[]{:S(2)}) copy-start(bf16[3,8,2,128,128]{4,3,2,1,0:T(8,128)(2,1)} %param.10) | copy-start | bytes 4718596
  2.5 64.3 %collective-permute-start = (bf16[8,72,256]{2,1,0:T(8,128)(2,1)}, bf16[8,72,256]{2,1,0:T(8,128)(2,1)S(1)}, u32[]{:S(2)}, u32[]{:S(2)}) collective-permute-start(bf16[8,72,256]{2,1,0:T(8,128)(2,1)} %pad_maximum_fusion.1), channel_id=1, source_target_pairs={{0,256},{8,264},{16,272},{24,280},{32,288},{40,296},{48,304},{56,3... | collective-permute-start | bytes 884744 | tf_op jit(solution)/shard_map/ppermute | solution.py:11
  15.1 55.2 %collective-permute-start.1 = (bf16[8,64,256]{2,1,0:T(8,128)(2,1)}, bf16[8,64,256]{2,1,0:T(8,128)(2,1)}, u32[]{:S(2)}, u32[]{:S(2)}) collective-permute-start(bf16[8,64,256]{2,1,0:T(8,128)(2,1)} %slice.163), channel_id=1, source_target_pairs={{0,256},{8,264},{16,272},{24,280},{32,288},{40,296},{48,304},{56,3... | collective-permute-start | bytes 786440 | tf_op jit(solution)/shard_map/ppermute | solution.py:11
  17.0 12.1 %copy-start.18 = (f32[8,128]{1,0:T(8,128)S(1)}, f32[8,128]{1,0:T(8,128)}, u32[]{:S(2)}) copy-start(f32[8,128]{1,0:T(8,128)} %param.9) | copy-start | bytes 12292
  17.5 86.7 %collective-permute-start.2 = (bf16[8,136,256]{2,0,1:T(8,128)(2,1)S(1)}, bf16[8,136,256]{2,0,1:T(8,128)(2,1)}, u32[]{:S(2)}, u32[]{:S(2)}) collective-permute-start(bf16[8,136,256]{2,0,1:T(8,128)(2,1)S(1)} %pad_maximum_fusion), channel_id=1, source_target_pairs={{0,64},{8,72},{16,80},{24,88},{32,96},{40,104},{48,112},{56,120},{... | collective-permute-start | bytes 1671176 | tf_op jit(solution)/shard_map/ppermute | solution.py:11
  24.1 35.4 %collective-permute-start.5 = (bf16[8,128,128]{2,1,0:T(8,128)(2,1)}, bf16[8,128,128]{2,1,0:T(8,128)(2,1)}, u32[]{:S(2)}, u32[]{:S(2)}) collective-permute-start(bf16[8,128,128]{2,1,0:T(8,128)(2,1)} %fusion.45), channel_id=1, source_target_pairs={{0,64},{8,72},{16,80},{24,88},{32,96},{40,104},{48,112},{56,120},{... | collective-permute-start | bytes 786440 | tf_op jit(solution)/shard_map/ppermute | solution.py:11
  35.7 33.8 %copy-start.6 = (bf16[8,128,128]{2,1,0:T(8,128)(2,1)S(1)}, bf16[8,128,128]{2,1,0:T(8,128)(2,1)}, u32[]{:S(2)}) copy-start(bf16[8,128,128]{2,1,0:T(8,128)(2,1)} %fusion.87) | copy-start | bytes 786436
  35.7 33.8 %copy-start.10 = (bf16[8,128,128]{2,1,0:T(8,128)(2,1)S(1)}, bf16[8,128,128]{2,1,0:T(8,128)(2,1)}, u32[]{:S(2)}) copy-start(bf16[8,128,128]{2,1,0:T(8,128)(2,1)} %get-tuple-element.49) | copy-start | bytes 786436
  35.7 33.8 %copy-start.12 = (bf16[8,128,128]{2,1,0:T(8,128)(2,1)S(1)}, bf16[8,128,128]{2,1,0:T(8,128)(2,1)}, u32[]{:S(2)}) copy-start(bf16[8,128,128]{2,1,0:T(8,128)(2,1)} %get-tuple-element.50) | copy-start | bytes 786436
  35.7 33.8 %copy-start.27 = (f32[8,64,256]{2,1,0:T(8,128)S(1)}, f32[8,64,256]{2,1,0:T(8,128)}, u32[]{:S(2)}) copy-start(f32[8,64,256]{2,1,0:T(8,128)} %fusion.22) | copy-start | bytes 1572868
  59.5 16.8 %collective-permute-start.8 = (bf16[8,128,128]{2,1,0:T(8,128)(2,1)}, bf16[8,128,128]{2,1,0:T(8,128)(2,1)S(1)}, u32[]{:S(2)}, u32[]{:S(2)}) collective-permute-start(bf16[8,128,128]{2,1,0:T(8,128)(2,1)} %collective-permute-done.5), channel_id=1, source_target_pairs={{0,1},{1,0},{2,3},{3,2},{4,5},{5,4},{6,7},{7,6},{8,9},{9,8},{10,11... | collective-permute-start | bytes 786440 | tf_op jit(solution)/shard_map/ppermute | solution.py:11
  62.8 16.6 %collective-permute-start.6 = (bf16[8,128,128]{2,1,0:T(8,128)(2,1)}, bf16[8,128,128]{2,1,0:T(8,128)(2,1)S(1)}, u32[]{:S(2)}, u32[]{:S(2)}) collective-permute-start(bf16[8,128,128]{2,1,0:T(8,128)(2,1)} %collective-permute-done.5), channel_id=1, source_target_pairs={{0,3},{1,2},{2,1},{3,0},{4,7},{5,6},{6,5},{7,4},{8,11},{9,10},{10,... | collective-permute-start | bytes 786440 | tf_op jit(solution)/shard_map/ppermute | solution.py:11
  66.9 9.0 %copy-start.5 = (bf16[8,72,256]{2,1,0:T(8,128)(2,1)}, bf16[8,72,256]{2,1,0:T(8,128)(2,1)S(1)}, u32[]{:S(2)}) copy-start(bf16[8,72,256]{2,1,0:T(8,128)(2,1)S(1)} %collective-permute-done) | copy-start | bytes 884740
  66.9 12.6 %collective-permute-start.7 = (bf16[8,128,128]{2,1,0:T(8,128)(2,1)}, bf16[8,128,128]{2,1,0:T(8,128)(2,1)S(1)}, u32[]{:S(2)}, u32[]{:S(2)}) collective-permute-start(bf16[8,128,128]{2,1,0:T(8,128)(2,1)} %collective-permute-done.5), channel_id=1, source_target_pairs={{0,2},{1,3},{2,0},{3,1},{4,6},{5,7},{6,4},{7,5},{8,10},{9,11},{10,... | collective-permute-start | bytes 786440 | tf_op jit(solution)/shard_map/ppermute | solution.py:11
  70.3 22.4 %collective-permute-start.3 = (bf16[8,64,256]{2,1,0:T(8,128)(2,1)S(1)}, bf16[8,64,256]{2,1,0:T(8,128)(2,1)S(1)}, u32[]{:S(2)}, u32[]{:S(2)}) collective-permute-start(bf16[8,64,256]{2,1,0:T(8,128)(2,1)S(1)} %fusion), channel_id=1, source_target_pairs={{0,128},{8,136},{16,144},{24,152},{32,160},{40,168},{48,176},{56,1... | collective-permute-start | bytes 786440 | tf_op jit(solution)/shard_map/ppermute | solution.py:11
  76.2 21.1 %collective-permute-start.10 = (bf16[8,64,256]{2,1,0:T(8,128)(2,1)S(1)}, bf16[8,64,256]{2,1,0:T(8,128)(2,1)S(1)}, u32[]{:S(2)}, u32[]{:S(2)}) collective-permute-start(bf16[8,64,256]{2,1,0:T(8,128)(2,1)S(1)} %fusion.5), channel_id=1, source_target_pairs={{0,128},{8,136},{16,144},{24,152},{32,160},{40,168},{48,176},{56,1... | collective-permute-start | bytes 786440 | tf_op jit(solution)/shard_map/ppermute | solution.py:11
  93.1 19.3 %collective-permute-start.4 = (bf16[8,64,256]{2,1,0:T(8,128)(2,1)S(1)}, bf16[8,64,256]{2,1,0:T(8,128)(2,1)S(1)}, u32[]{:S(2)}, u32[]{:S(2)}) collective-permute-start(bf16[8,64,256]{2,1,0:T(8,128)(2,1)S(1)} %fusion.1), channel_id=1, source_target_pairs={{0,64},{8,72},{16,80},{24,88},{32,96},{40,104},{48,112},{56,120},{... | collective-permute-start | bytes 786440 | tf_op jit(solution)/shard_map/ppermute | solution.py:11
  98.0 22.2 %collective-permute-start.11 = (bf16[8,64,256]{2,1,0:T(8,128)(2,1)S(1)}, bf16[8,64,256]{2,1,0:T(8,128)(2,1)S(1)}, u32[]{:S(2)}, u32[]{:S(2)}) collective-permute-start(bf16[8,64,256]{2,1,0:T(8,128)(2,1)S(1)} %fusion.6), channel_id=1, source_target_pairs={{0,64},{8,72},{16,80},{24,88},{32,96},{40,104},{48,112},{56,120},{... | collective-permute-start | bytes 786440 | tf_op jit(solution)/shard_map/ppermute | solution.py:11
  117.0 16.5 %collective-permute-start.9 = (bf16[8,64,256]{2,1,0:T(8,128)(2,1)S(1)}, bf16[8,64,256]{2,1,0:T(8,128)(2,1)S(1)}, u32[]{:S(2)}, u32[]{:S(2)}) collective-permute-start(bf16[8,64,256]{2,1,0:T(8,128)(2,1)S(1)} %convolution_convert_fusion.3), channel_id=1, source_target_pairs={{0,128},{8,136},{16,144},{24,152},{32,160},{40,168},{48,176},{56,1... | collective-permute-start | bytes 786440 | tf_op jit(solution)/shard_map/ppermute | solution.py:11
  119.4 14.1 %copy-start.22 = (f32[8,64,256]{2,1,0:T(8,128)}, f32[8,64,256]{2,1,0:T(8,128)S(1)}, u32[]{:S(2)}) copy-start(f32[8,64,256]{2,1,0:T(8,128)S(1)} %fusion.99) | copy-start | bytes 1572868
  124.6 8.8 %copy-start.4 = (bf16[8,128,256]{2,1,0:T(8,128)(2,1)S(1)}, bf16[8,128,256]{2,1,0:T(8,128)(2,1)}, u32[]{:S(2)}) copy-start(bf16[8,128,256]{2,1,0:T(8,128)(2,1)} %param.8) | copy-start | bytes 1572868
  124.6 8.8 %copy-start.9 = (bf16[8,128,128]{2,1,0:T(8,128)(2,1)S(1)}, bf16[8,128,128]{2,1,0:T(8,128)(2,1)}, u32[]{:S(2)}) copy-start(bf16[8,128,128]{2,1,0:T(8,128)(2,1)} %copy-done.8) | copy-start | bytes 786436
  124.7 8.8 %copy-start.15 = (bf16[8,128,128]{2,1,0:T(8,128)(2,1)S(1)}, bf16[8,128,128]{2,1,0:T(8,128)(2,1)}, u32[]{:S(2)}) copy-start(bf16[8,128,128]{2,1,0:T(8,128)(2,1)} %copy-done.14) | copy-start | bytes 786436
  124.7 8.8 %copy-start.17 = (bf16[8,128,128]{2,1,0:T(8,128)(2,1)S(1)}, bf16[8,128,128]{2,1,0:T(8,128)(2,1)}, u32[]{:S(2)}) copy-start(bf16[8,128,128]{2,1,0:T(8,128)(2,1)} %copy-done.16) | copy-start | bytes 786436
  124.7 15.5 %collective-permute-start.12 = (bf16[8,64,256]{2,1,0:T(8,128)(2,1)S(1)}, bf16[8,64,256]{2,1,0:T(8,128)(2,1)S(1)}, u32[]{:S(2)}, u32[]{:S(2)}) collective-permute-start(bf16[8,64,256]{2,1,0:T(8,128)(2,1)S(1)} %convolution_convert_fusion), channel_id=1, source_target_pairs={{0,128},{8,136},{16,144},{24,152},{32,160},{40,168},{48,176},{56,1... | collective-permute-start | bytes 786440 | tf_op jit(solution)/shard_map/ppermute | solution.py:11
  129.3 10.9 %copy-start.24 = (f32[8,64,256]{2,1,0:T(8,128)}, f32[8,64,256]{2,1,0:T(8,128)S(1)}, u32[]{:S(2)}) copy-start(f32[8,64,256]{2,1,0:T(8,128)S(1)} %fusion.97) | copy-start | bytes 1572868
  134.0 6.8 %slice-start = ((bf16[8,72,256]{2,1,0:T(8,128)(2,1)}), bf16[8,64,256]{2,1,0:T(8,128)(2,1)S(1)}, s32[]{:S(2)}) async-start(bf16[8,72,256]{2,1,0:T(8,128)(2,1)} %copy-done.5), calls=%async_computation.1 | async-start | bytes 524288 | tf_op jit(solution)/shard_map/slice | solution.py:114
  134.0 6.8 %copy-start.7 = (bf16[8,128,128]{2,1,0:T(8,128)(2,1)S(1)}, bf16[8,128,128]{2,1,0:T(8,128)(2,1)}, u32[]{:S(2)}) copy-start(bf16[8,128,128]{2,1,0:T(8,128)(2,1)} %fusion.87) | copy-start | bytes 786436
  134.0 6.8 %copy-start.11 = (bf16[8,128,128]{2,1,0:T(8,128)(2,1)S(1)}, bf16[8,128,128]{2,1,0:T(8,128)(2,1)}, u32[]{:S(2)}) copy-start(bf16[8,128,128]{2,1,0:T(8,128)(2,1)} %get-tuple-element.49) | copy-start | bytes 786436
  134.0 6.8 %copy-start.13 = (bf16[8,128,128]{2,1,0:T(8,128)(2,1)S(1)}, bf16[8,128,128]{2,1,0:T(8,128)(2,1)}, u32[]{:S(2)}) copy-start(bf16[8,128,128]{2,1,0:T(8,128)(2,1)} %get-tuple-element.50) | copy-start | bytes 786436
  (10 other events, 28.7 us)
